TPU v7x, 128 devices: a whole 4x4x4 slice. The times are simulated.
128 devices in a mesh: tm: 4 (over x_hi, core), slope: 32 (over x_lo, z, y).
Axes of the slice: x: 4 (x_hi: 2, x_lo: 2; x = x_hi * 2 + x_lo), y: 4, z: 4, core: 2. Of those that a mesh axis runs over, the one named last changes fastest.
Arguments:
- telemetry: bfloat16 [32, 32, 96, 4096], P('slope', None, None, 'tm'), may hold values from -24 to 24
- frame_ids: int32 [4096], P('tm'), may hold values from 0 to 1023, as said below
- valid: int32 [8, 48], replicated, may hold values 0 or 1
- noise: float32 [1024], replicated, may hold values from 0.1 to 1
- prior_next: float32 [32, 32, 96, 1024], P('slope', 'tm'), may hold values from -2 to 2
Outputs:
- panel: float32 [32, 32, 96, 1024], P('slope', 'tm')
- next_block: float32 [32, 32, 96, 1024], P('slope', 'tm')
Inputs may be any that keep to these rules, and one draw needn't show every extreme that they name: `frame_ids`: entry f names a frame of the block of 1024 buffer frames that starts at (f // 1024) * 1024; entries may repeat.
All inputs are finite; a program needn't handle non-finite values.
Results may differ from a plain program's by a relative error of at most 0.0003.
Values may be sent and summed in bfloat16 or wider, within the bound.
No kernel may reach another device: no remote copies, remote signals or barrier semaphores. Data moves between devices by JAX's collectives and lax.ppermute only.
A program may use at most 128 MiB of HBM per device.

v0:
```python
import jax
import jax.numpy as jnp
from jax import lax
from jax.sharding import PartitionSpec as P


def shards(telemetry, frame_ids, valid, noise, prior_next):
    slope_count = lax.axis_size("slope")
    tm_count = lax.axis_size("tm")
    slope_index = lax.axis_index("slope")
    tm_index = lax.axis_index("tm")
    row_block = telemetry.shape[1]
    cycles = telemetry.shape[2]
    block_width = noise.shape[0]
    quarter = row_block // tm_count
    frames_total = frame_ids.shape[0] * tm_count
    rows_iota = lax.broadcasted_iota(jnp.int32, (row_block, cycles), 0)
    cycle_iota = lax.broadcasted_iota(jnp.int32, (row_block, cycles), 1)
    slope_ids = (cycle_iota * slope_count + slope_index) * row_block + rows_iota
    sensors, segments = valid.shape
    per_sensor = cycles * block_width // sensors
    seg_len = per_sensor // segments
    seg_codes = slope_ids // per_sensor * segments + slope_ids % per_sensor // seg_len
    labels = jnp.arange(sensors * segments, dtype=jnp.int32)
    keep_row = jnp.sum(jnp.where(seg_codes[:, :, None] == labels, valid.reshape(-1), 0), axis=2)
    selected = jnp.take(telemetry[0], frame_ids, axis=2) * keep_row[:, :, None].astype(jnp.bfloat16)
    first_cols = lax.all_gather(selected[:, 0, :], "slope", axis=0, tiled=True)
    gram_block = lax.psum_scatter(
        jnp.einsum("rcf,jf->rcj", selected, first_cols, preferred_element_type=jnp.float32),
        "tm",
        scatter_dimension=0,
        tiled=True,
    )
    diag_cols = lax.broadcasted_iota(jnp.int32, (quarter, block_width), 1)
    diag_ids = (
        slope_index * row_block
        + tm_index * quarter
        + lax.broadcasted_iota(jnp.int32, (quarter, block_width), 0)
    )
    first_block = gram_block / float(frames_total)
    first_block = first_block.at[:, 0, :].add(jnp.where(diag_cols == diag_ids, noise[None, :], 0.0))
    lead_rows = lax.all_gather(first_block[:, 0, :], "tm", axis=0, tiled=True)
    diag_block = lax.all_gather(lead_rows, "slope", axis=0, tiled=True)
    factor = jnp.linalg.cholesky(diag_block)
    inverse = jax.scipy.linalg.solve_triangular(
        factor, jnp.eye(block_width, dtype=jnp.float32), lower=True
    )
    panel_rows = jnp.einsum("rcj,kj->rck", first_block, inverse, precision=lax.Precision.HIGHEST)
    second_part = lax.all_gather(panel_rows[:, 1, :], "tm", axis=0, tiled=True)
    second = lax.all_gather(second_part, "slope", axis=0, tiled=True)
    update = jnp.einsum("rci,ji->rcj", panel_rows, second, precision=lax.Precision.HIGHEST)
    next_block = prior_next[0] - update
    return (panel_rows[None], next_block[None])


def solution(mesh):
    return jax.shard_map(
        shards,
        mesh=mesh,
        in_specs=(P("slope", None, None, "tm"), P("tm"), P(), P(), P("slope", "tm", None, None)),
        out_specs=(P("slope", "tm", None, None), P("slope", "tm", None, None)),
        check_vma=False,
    )
```

profile of v0, /device:TPU:0, one launch (start us, length us, event | category | flops | bytes accessed | tf_op | source)
XLA Modules:
  0.0 1056.5 jit_solution(5433149243519154248)
XLA Ops:
  10.8 12.0 %copy.26 = bf16[1,32,96,1024]{2,1,3,0:T(8,128)(2,1)} copy(bf16[1,32,96,1024]{3,2,1,0:T(8,128)(2,1)} %param.7) | data formatting | bytes 12582912 | tf_op args[0]
  22.8 13.3 %gather_fusion = bf16[1024,32,96]{2,1,0:T(8,128)(2,1)} fusion(bf16[32,96,1024]{1,0,2:T(8,128)(2,1)} %bitcast.128, s32[1024]{0:T(1024)S(1)} %fusion.93), kind=kCustom, calls=%fused_computation | custom fusion | bytes 12587008 | tf_op jit(solution)/shard_map/jit(_take)/gather | solution.py:26
  36.0 13.1 %copy.27 = bf16[1024,32,96]{0,1,2:T(8,128)(2,1)} copy(bf16[1024,32,96]{2,1,0:T(8,128)(2,1)} %gather_fusion) | data formatting | bytes 12582912 | tf_op jit(solution)/shard_map/jit(_take)/gather | solution.py:26
  56.2 155.3 %all-gather.9.cloned.1.call-done = bf16[1024,1,1024]{2,0,1:T(8,128)(2,1)} async-done(((bf16[32,1,1024]{2,0,1:T(8,128)(2,1)}), bf16[1024,1,1024]{2,0,1:T(8,128)(2,1)}) %all-gather.9.cloned.1.call-update) | async-done | bytes 2097168 | tf_op jit(solution)/shard_map/all_gather | solution.py:27
  211.5 15.0 %fusion = f32[32,96,1024]{2,1,0:T(8,128)} fusion(bf16[32,96,1024]{2,0,1:T(8,128)(2,1)} %copy-done.4, bf16[1024,1,1024]{2,0,1:T(8,128)(2,1)} %all-gather.9.cloned.1.call-done), kind=kOutput, calls=%fused_computation.3 | convolution fusion | flops 6442450944 | bytes 20971520 | tf_op jit(solution)/shard_map/rcf,jf->rcj/dot_general | solution.py:29
  226.6 106.9 %reduce-scatter.2.cloned.1.call-done = f32[8,96,1024]{2,1,0:T(8,128)} async-done(((f32[32,96,1024]{2,1,0:T(8,128)}), f32[8,96,1024]{2,1,0:T(8,128)}) %reduce-scatter.2.cloned.1.call-update) | async-done | bytes 3145744 | tf_op jit(solution)/shard_map/reduce_scatter | solution.py:28
  335.8 7.4 all-gather.1
  347.2 152.2 %all-gather.11.cloned.1.call-done = f32[1024,1,1024]{2,1,0:T(1,128)} async-done(((f32[32,1,1024]{2,1,0:T(1,128)}), f32[1024,1,1024]{2,1,0:T(1,128)}) %all-gather.11.cloned.1.call-update) | async-done | bytes 4194320 | tf_op jit(solution)/shard_map/all_gather | solution.py:43
  499.4 11.1 %copy.30 = f32[1024,1,1024]{0,2,1:T(8,128)} copy(f32[1024,1,1024]{2,1,0:T(1,128)} %all-gather.11.cloned.1.call-done) | data formatting | bytes 8388608 | tf_op jit(solution)/shard_map/all_gather | solution.py:43
  510.5 5.0 fusion.5
  517.5 11.7 %cholesky.223 = f32[128,128]{1,0:T(8,128)S(1)} custom-call(f32[128,128]{1,0:T(8,128)S(1)} %cholesky.580), custom_call_target="Cholesky" | custom-call | tf_op jit(solution)/shard_map/jit(cholesky)/cholesky | solution.py:44
  529.3 9.8 custom-call.63
  545.5 12.1 %cholesky.244 = f32[128,128]{1,0:T(8,128)S(1)} custom-call(f32[128,128]{1,0:T(8,128)S(1)} %cholesky.584), custom_call_target="Cholesky" | custom-call | tf_op jit(solution)/shard_map/jit(cholesky)/cholesky | solution.py:44
  558.2 9.8 custom-call.64
  571.4 11.7 %cholesky.468 = f32[128,128]{1,0:T(8,128)S(1)} custom-call(f32[128,128]{1,0:T(8,128)S(1)} %cholesky.589), custom_call_target="Cholesky" | custom-call | tf_op jit(solution)/shard_map/jit(cholesky)/cholesky | solution.py:44
  584.4 9.8 custom-call.65
  597.7 11.9 %cholesky.487 = f32[128,128]{1,0:T(8,128)S(1)} custom-call(f32[128,128]{1,0:T(8,128)S(1)} %cholesky.594), custom_call_target="Cholesky" | custom-call | tf_op jit(solution)/shard_map/jit(cholesky)/cholesky | solution.py:44
  610.9 9.8 custom-call.66
  624.2 11.7 %cholesky.506 = f32[128,128]{1,0:T(8,128)S(1)} custom-call(f32[128,128]{1,0:T(8,128)S(1)} %cholesky.599), custom_call_target="Cholesky" | custom-call | tf_op jit(solution)/shard_map/jit(cholesky)/cholesky | solution.py:44
  637.3 10.0 custom-call.67
  650.6 11.7 %cholesky.526 = f32[128,128]{1,0:T(8,128)S(1)} custom-call(f32[128,128]{1,0:T(8,128)S(1)} %cholesky.604), custom_call_target="Cholesky" | custom-call | tf_op jit(solution)/shard_map/jit(cholesky)/cholesky | solution.py:44
  663.6 9.8 custom-call.68
  676.4 12.1 %cholesky.546 = f32[128,128]{1,0:T(8,128)S(1)} custom-call(f32[128,128]{1,0:T(8,128)S(1)} %cholesky.609), custom_call_target="Cholesky" | custom-call | tf_op jit(solution)/shard_map/jit(cholesky)/cholesky | solution.py:44
  689.9 9.8 custom-call.69
  702.3 11.7 %cholesky.564 = f32[128,128]{1,0:T(8,128)S(1)} custom-call(f32[128,128]{1,0:T(8,128)S(1)} %convolution_subtract_fusion.11), custom_call_target="Cholesky" | custom-call | tf_op jit(solution)/shard_map/jit(cholesky)/cholesky | solution.py:44
  721.1 4.8 select_select_fusion
  725.9 27.3 %while.2 = (s32[]{:T(128)}, f32[1024,1024]{1,0:T(8,128)}, s32[8,2]{0,1:T(2,128)S(1)}, f32[8,128,128]{2,1,0:T(8,128)}, s32[]{:T(128)}) while((s32[]{:T(128)}, f32[1024,1024]{1,0:T(8,128)}, s32[8,2]{0,1:T(2,128)S(1)}, f32[8,128,128]{2,1,0:T(8,128)}, s32[]{:T(128)}) %tuple.67), condition=%wide.while_cond.1, body=%wide.while_body.1.sunk | while | flops 2 | bytes 132205 | solution.py:45
  753.2 79.6 %custom-call.70 = f32[8,128,128]{1,2,0:T(8,128)S(1)} custom-call(f32[8,128,128]{2,1,0:T(8,128)} %get-tuple-element.21), custom_call_target="InvertDiagBlocksLowerTriangular" | custom-call | tf_op jit(solution)/shard_map/jit(_solve_triangular)/triangular_solve | solution.py:45
  856.1 11.7 %fusion.6 = f32[8,96,1024]{2,0,1:T(8,128)S(1)} fusion(f32[1024,1024]{1,0:T(8,128)S(1)} %convolution_dynamic-update-slice_fusion, f32[8,96,1024]{2,1,0:T(8,128)S(1)} %copy-done.2), kind=kOutput, calls=%fused_computation.14 | convolution fusion | flops 9663676416 | bytes 10485760 | tf_op jit(solution)/shard_map/rcj,kj->rck/dot_general | solution.py:48
  867.8 7.6 all-gather.3
  879.0 153.4 %all-gather.13.cloned.1.call-done = f32[1024,1,1024]{2,1,0:T(1,128)} async-done(((f32[32,1,1024]{2,1,0:T(1,128)}), f32[1024,1,1024]{2,1,0:T(1,128)}) %all-gather.13.cloned.1.call-update) | async-done | bytes 4194320 | tf_op jit(solution)/shard_map/all_gather | solution.py:50
  1032.4 17.1 %fusion.8 = f32[1,8,96,1024]{3,2,1,0:T(8,128)} fusion(f32[1,8,96,1024]{3,2,1,0:T(8,128)} %param.11, f32[1024,1,1024]{2,1,0:T(1,128)} %all-gather.13.cloned.1.call-done, f32[8,96,1024]{2,0,1:T(8,128)S(1)} %fusion.6), kind=kOutput, calls=%fused_computation.19 | convolution fusion | flops 9664462848 | bytes 13631488 | tf_op jit(solution)/shard_map/rci,ji->rcj/dot_general | solution.py:51
  (118 shorter events, 107.8 us)
Async XLA Ops:
  7.2 204.3 %all-gather.9.cloned.1.call-start = ((), (), s32[]{:S(2)}) async-start(), calls=%async_computation.2 | async-start | bytes 2162688 | tf_op jit(solution)/shard_map/all_gather | solution.py:27
  52.9 2.6 copy-start.4
  56.1 277.4 %reduce-scatter.2.cloned.1.call-start = ((), (), s32[]{:S(2)}) async-start(), calls=%async_computation.1 | async-start | bytes 15728640 | tf_op jit(solution)/shard_map/reduce_scatter | solution.py:28
  226.5 109.2 %copy-start.5 = (f32[1024]{0:T(1024)S(1)}, f32[1024]{0:T(1024)}, u32[]{:S(2)}) copy-start(f32[1024]{0:T(1024)} %param.10) | copy-start | bytes 12292
  226.5 272.8 %all-gather.11.cloned.1.call-start = ((), (), s32[]{:S(2)}) async-start(), calls=%async_computation.3 | async-start | bytes 4325376 | tf_op jit(solution)/shard_map/all_gather | solution.py:43
  343.2 689.2 %all-gather.13.cloned.1.call-start = ((), (), s32[]{:S(2)}) async-start(), calls=%async_computation.4 | async-start | bytes 4325376 | tf_op jit(solution)/shard_map/all_gather | solution.py:50
  347.1 163.4 %copy-start.1 = (f32[8,96,1024]{2,1,0:T(8,128)}, f32[8,96,1024]{2,1,0:T(8,128)S(1)}, u32[]{:S(2)}) copy-start(f32[8,96,1024]{2,1,0:T(8,128)S(1)} %scatter-add.4) | copy-start | bytes 9437188
  515.5 2.0 copy-start.3
  832.8 3.9 copy-start
  851.0 5.1 copy-start.2
Sparse Core Ops, SparseCore 0:
  56.3 155.1 all-gather.8
  226.7 106.8 reduce-scatter.1
  343.3 155.9 all-gather.10
  875.6 156.7 all-gather.12
where the time goes:
time: 1060 us
  waiting for transfers between devices  568 us (54%)
  other arithmetic  275 us (26%)
  matrix products  90.1 us (8%)
  local copies, waits for them, and re-layouts  89 us (8%)
  between operations  19.7 us (2%)
  blocking collectives  15 us (1%)
    another operation x30, other arithmetic, shards(): factor = jnp.linalg.cholesky(diag_block)  173 us
    all_gather x1, waiting for transfers between devices, shards(): first_cols = lax.all_gather(selected[:, 0, :], 'slope', axis=0, tiled=True)  155 us
    all_gather x1, waiting for transfers between devices, shards(): second = lax.all_gather(second_part, 'slope', axis=0, tiled=True)  153 us
    all_gather x1, waiting for transfers between devices, shards(): diag_block = lax.all_gather(lead_rows, 'slope', axis=0, tiled=True)  152 us
    reduce_scatter x1, waiting for transfers between devices, shards(): lax.psum_scatter(jnp.einsum('rcf,jf->rcj', selected, first_cols, preferre...  107 us
    another operation x3, other arithmetic, shards(): jax.scipy.linalg.solve_triangular(factor, jnp.eye(block_width, dtype=jnp....  84.4 us
    another operation x24, local copies, waits for them, and re-layouts  27.3 us
    gather x2, local copies, waits for them, and re-layouts, shards(): jnp.take(telemetry[0], frame_ids, axis=2)  26.3 us
  transfers between devices with their start and end apart: 4, of which 4 were waited for; matrix products, arithmetic and copies ran while one was open for 1% of the time, Pallas kernels for 0%

commit v1 on v0

v1 whole, which is shorter than its diff:
```python
import jax
import jax.numpy as jnp
from jax import lax
from jax.experimental import pallas as pl
from jax.experimental.pallas import tpu as pltpu
from jax.sharding import PartitionSpec as P

NB = 128
MB = 8
TN = (((0,), (0,)), ((), ()))
NT = (((1,), (1,)), ((), ()))
WHOLE = pl.BlockSpec(memory_space=pltpu.VMEM)


def params(mib=40):
    return pltpu.CompilerParams(vmem_limit_bytes=mib * 2**20)


def bf16_round(z):
    return z.astype(jnp.bfloat16).astype(jnp.float32)


def split3(z):
    high = bf16_round(z)
    rest = z - high
    mid = bf16_round(rest)
    return high, mid, rest - mid


def row_of(z, j):
    return jnp.broadcast_to(z[j:j + 1, :], z.shape)


def factor_block(wa, wx, out):
    sub = lax.broadcasted_iota(jnp.int32, (MB, NB), 0)
    a = wa[0:MB, :]
    x = wx[0:MB, :]
    for k in range(NB // MB):
        lo = MB * k
        after = lo + MB < NB
        cols = [jnp.broadcast_to(a[:, lo + j:lo + j + 1], (MB, NB)) for j in range(MB)]
        if after:
            na = wa[lo + MB:lo + 2 * MB, :]
            nx = wx[lo + MB:lo + 2 * MB, :]
            ncols = [jnp.broadcast_to(na[:, lo + j:lo + j + 1], (MB, NB)) for j in range(MB)]
        inv_d = jnp.zeros((MB, NB), jnp.float32)
        piv = jnp.zeros((MB, NB), jnp.float32)
        for j in range(MB):
            pivot = row_of(cols[j], j)
            recip = 1.0 / pivot
            mult = jnp.where(sub > j, cols[j] * recip, 0.0)
            ra, rx = row_of(a, j), row_of(x, j)
            if after:
                nmult = ncols[j] * recip
                na = na - nmult * ra
                nx = nx - nmult * rx
            for l in range(j + 1, MB):
                rc = row_of(cols[l], j)
                cols[l] = cols[l] - mult * rc
                if after:
                    ncols[l] = ncols[l] - nmult * rc
            a = a - mult * ra
            x = x - mult * rx
            inv_d = jnp.where(sub == j, recip, inv_d)
            piv = jnp.where(sub == j, pivot, piv)
        out[lo:lo + MB, :] = x * (1.0 / jnp.sqrt(piv))
        if lo + 2 * MB < NB:
            top = lo + 2 * MB
            right = jnp.concatenate([a * inv_d, x * inv_d], axis=1)
            lh, lm, ll = split3(a)
            rh, rm, rl = split3(right)
            left_stack = jnp.concatenate([lh, lh, lm, lh, ll, lm], axis=0).astype(jnp.bfloat16)
            right_stack = jnp.concatenate([rh, rm, rh, rl, rh, rm], axis=0).astype(jnp.bfloat16)
            prod = lax.dot_general(left_stack, right_stack, TN, preferred_element_type=jnp.float32)
            wa[top:, :] = wa[top:, :] - prod[top:, :NB]
            wx[top:, :] = wx[top:, :] - prod[top:, NB:]
        if after:
            a, x = na, nx


def chol_panels(first, count, big, wa, wx, linv, ys):
    n = big.shape[0]
    nblk = n // NB
    rows = lax.broadcasted_iota(jnp.int32, (NB, NB), 0)
    lanes = lax.broadcasted_iota(jnp.int32, (NB, NB), 1)
    eye = jnp.where(rows == lanes, 1.0, 0.0)

    def panel_step(p, carry):
        at = pl.multiple_of(p * NB, NB)
        wa[...] = big[pl.ds(at, NB), pl.ds(at, NB)]
        wx[...] = eye
        big[pl.ds(at, NB), pl.ds(at, NB)] = eye
        factor_block(wa, wx, linv)
        y = jnp.dot(linv[...], big[pl.ds(at, NB), :], precision=lax.Precision.HIGHEST, preferred_element_type=jnp.float32)
        big[pl.ds(at, NB), :] = y
        high, mid, low = (part.astype(jnp.bfloat16) for part in split3(y))
        for i, part in enumerate((high, mid, low, high)):
            ys[i * NB:(i + 1) * NB, :] = part

        def trail(i, c):
            row = pl.multiple_of(i * NB, NB)
            big[pl.ds(row, NB), pl.ds(at, NB)] = jnp.zeros((NB, NB), jnp.float32)
            hm = ys[0:2 * NB, pl.ds(row, NB)]
            mh = jnp.concatenate([ys[NB:2 * NB, pl.ds(row, NB)], ys[0:NB, pl.ds(row, NB)]], axis=0)
            lh = ys[2 * NB:4 * NB, pl.ds(row, NB)]
            hl = jnp.concatenate([ys[0:NB, :], ys[2 * NB:3 * NB, :]], axis=0)
            dot = lambda u, v: lax.dot_general(u, v, TN, preferred_element_type=jnp.float32)
            upd = dot(hm, ys[0:2 * NB, :]) + (dot(mh, ys[0:2 * NB, :]) + dot(lh, hl))
            big[pl.ds(row, NB), :] = big[pl.ds(row, NB), :] - upd
            return c

        lax.fori_loop(p + 1, nblk, trail, 0)
        return carry

    lax.fori_loop(first, first + count, panel_step, 0)


CHOL_SCRATCH = [pltpu.VMEM((NB, NB), jnp.float32)] * 3


def chol_step(big, first, count):
    n = big.shape[0]

    def kernel(src, dst, wa, wx, linv, ys):
        chol_panels(first, count, dst, wa, wx, linv, ys)

    return pl.pallas_call(
        kernel, out_shape=jax.ShapeDtypeStruct(big.shape, jnp.float32), in_specs=[WHOLE], out_specs=WHOLE,
        scratch_shapes=CHOL_SCRATCH + [pltpu.VMEM((4 * NB, n), jnp.bfloat16)], input_output_aliases={0: 0},
        compiler_params=params(), name="chol_panels")(big)


SPLIT = (2, 5, 1)
AXES = ("tm", "slope")
RING = 4
SCALARS = pl.BlockSpec(memory_space=pltpu.SMEM)


def pick_first(tel, ids, keep, core):
    rows, _, frames = tel.shape
    half = rows // 2

    def kernel(core_ref, tel_ref, ids_ref, keep_ref, mine_ref, theirs_ref, second_ref, hot_ref, got, lead):
        hot_ref[...] = jnp.where(lax.broadcasted_iota(jnp.int32, (frames, frames), 0) == ids_ref[...], 1.0, 0.0).astype(jnp.bfloat16)
        got[...] = jnp.dot(tel_ref[...].reshape(rows * 16, frames), hot_ref[...], preferred_element_type=jnp.float32).reshape(rows, 16, frames)
        lead[...] = got[:, 0, :] * keep_ref[0:1, 0:1]
        at = pl.multiple_of(core_ref[0] * half, half)
        mine_ref[...] = lead[pl.ds(at, half), :].astype(jnp.bfloat16)
        theirs_ref[...] = lead[pl.ds(pl.multiple_of(half - at, half), half), :].astype(jnp.bfloat16)
        second_ref[...] = (got[:, 1, :] * keep_ref[1:2, 0:1]).astype(jnp.bfloat16)

    whole = lambda shape: pl.BlockSpec(shape, lambda i: (0,) * len(shape))
    shapes = ((half, frames), (half, frames), (rows, frames), (frames, frames))
    return pl.pallas_call(
        kernel,
        grid=(1,),
        out_shape=tuple(jax.ShapeDtypeStruct(s, jnp.bfloat16) for s in shapes),
        in_specs=[SCALARS, pl.BlockSpec((rows, 16, frames), lambda i: (0, 0, 0)), whole((1, frames)), whole(keep.shape)],
        out_specs=tuple(whole(s) for s in shapes),
        scratch_shapes=[pltpu.VMEM((rows, 16, frames), jnp.float32), pltpu.VMEM((rows, frames), jnp.float32)],
        compiler_params=params(), name="pick_first")(core, tel, ids, keep)


def pick_all(tel, hot, keep, tm_index):
    rows, cycles, frames = tel.shape
    per = 4
    quarter = rows // RING
    steps = quarter // per

    def kernel(tm_ref, tel_ref, hot_ref, keep_ref, *outs):
        got = jnp.dot(tel_ref[...].reshape(per * cycles, frames), hot_ref[...], preferred_element_type=jnp.float32)
        got = (got.reshape(per, cycles, frames) * keep_ref[...][None]).astype(jnp.bfloat16)
        for k in range(RING):
            @pl.when(pl.program_id(0) // steps == k)
            def _():
                outs[k][...] = got

    place = lambda k: pl.BlockSpec((per, cycles, frames), lambda i, tm: (jnp.clip(i - steps * k, 0, steps - 1), 0, 0))
    return pl.pallas_call(
        kernel, out_shape=(jax.ShapeDtypeStruct((quarter, cycles, frames), jnp.bfloat16),) * RING,
        grid_spec=pltpu.PrefetchScalarGridSpec(
            num_scalar_prefetch=1, grid=(rows // per,),
            in_specs=[pl.BlockSpec((per, cycles, frames), lambda i, tm: (jnp.bitwise_xor(tm[0], i // steps) * steps + i % steps, 0, 0)),
                      pl.BlockSpec((frames, frames), lambda i, tm: (0, 0)), pl.BlockSpec(keep.shape, lambda i, tm: (0, 0))],
            out_specs=tuple(place(k) for k in range(RING))),
        compiler_params=params(), name="pick_all")(tm_index, tel, hot, keep)


def lead_gram(own, other, second_rows, noise, place):
    width = noise.shape[1]
    tm_count, quarter, frames = second_rows.shape
    half = own[0].shape[3]
    scale = 1.0 / (tm_count * frames)
    group = 2 * RING

    def kernel(place_ref, *refs):
        parts = (refs[:RING], refs[RING:2 * RING])
        rows_ref, noise_ref, cols_hbm, gram_ref, second_ref, left, acc, arrive, leave = refs[2 * RING:]
        me_core, me_x, me_y, me_z = (place_ref[i] for i in range(4))

        def fetch(t, slot):
            x_hi, c = t // 2, t % 2
            for kind in range(2):
                by = me_core if kind == 0 else 1 - me_core
                on_z = by == 0
                outer_me, inner_me = jnp.where(on_z, me_z, me_y), jnp.where(on_z, me_y, me_z)
                outer_step, inner_step = jnp.where(on_z, width // 8, width // 32), jnp.where(on_z, width // 32, width // 8)
                shift_c = (by + c) % 2
                for x_lo in range(2):
                    shift_x = (me_x + RING - x_hi * 2 - x_lo) % RING
                    for i in range(RING):
                        for q in range(RING):
                            at = x_lo * (width // 2) + ((outer_me + RING - i) % RING) * outer_step + ((inner_me + RING - q) % RING) * inner_step + by * half
                            pltpu.make_async_copy(parts[kind][i].at[q, shift_x, shift_c], left.at[slot, pl.ds(pl.multiple_of(at, half), half)], arrive.at[slot]).start()

        def out_copy(t, slot):
            return pltpu.make_async_copy(left.at[slot, pl.ds(0, width)], cols_hbm.at[t], leave.at[slot])

        for slot in range(2):
            left[slot, width:, :] = jnp.zeros((16, frames), jnp.bfloat16)
        fetch(0, 0)

        def one(t, carry):
            slot = t % 2

            @pl.when(jnp.logical_and(t >= 1, t + 1 < tm_count))
            def _():
                out_copy(t - 1, 1 - slot).wait()

            @pl.when(t + 1 < tm_count)
            def _():
                fetch(t + 1, 1 - slot)

            pltpu.make_async_copy(cols_hbm.at[0], left.at[slot, pl.ds(0, width)], arrive.at[slot]).wait()
            left[slot, width:width + quarter, :] = rows_ref[t]
            out_copy(t, slot).start()
            part = lax.dot_general(left[slot], left[slot, :width, :], NT, preferred_element_type=jnp.float32)

            @pl.when(t == 0)
            def _():
                acc[...] = part

            @pl.when(t > 0)
            def _():
                acc[...] += part

            return carry

        lax.fori_loop(0, tm_count, one, 0)
        rows = lax.broadcasted_iota(jnp.int32, (width, width), 0)
        diag = rows == lax.broadcasted_iota(jnp.int32, (width, width), 1)
        gram_ref[...] = acc[:width, :] * scale + jnp.where(diag, noise_ref[...], 0.0)
        second = acc[width:width + quarter, :] * scale
        for i in range(group):
            second_ref[i] = second
        out_copy(tm_count - 2, 0).wait()
        out_copy(tm_count - 1, 1).wait()

    anywhere = pl.BlockSpec(memory_space=pl.ANY)
    return pl.pallas_call(
        kernel,
        out_shape=(jax.ShapeDtypeStruct((tm_count, width, frames), jnp.bfloat16), jax.ShapeDtypeStruct((width, width), jnp.float32),
                   jax.ShapeDtypeStruct((group, quarter, width), jnp.float32)),
        in_specs=[SCALARS] + [anywhere] * (2 * RING) + [WHOLE] * 2,
        out_specs=(anywhere, WHOLE, WHOLE),
        scratch_shapes=[pltpu.VMEM((2, width + 16, frames), jnp.bfloat16), pltpu.VMEM((width + 16, width), jnp.float32),
                        pltpu.SemaphoreType.DMA((2,)), pltpu.SemaphoreType.DMA((2,))],
        compiler_params=params(40), name="lead_gram")(place, *own, *other, second_rows, noise)


def two(z):
    high = z.astype(jnp.bfloat16)
    return high, (z - high.astype(jnp.float32)).astype(jnp.bfloat16)


def dot3(left, right):
    dot = lambda p, q: lax.dot_general(p, q, NT, preferred_element_type=jnp.float32)
    return dot(left[0], right[0]) + (dot(left[0], right[1]) + dot(left[1], right[0]))


STRIPS = 4


def lower_dot3(left_refs, right_refs, put):
    n = right_refs[0].shape[0]
    step = n // STRIPS
    for s in range(STRIPS):
        rows, k = pl.ds(s * step, step), (s + 1) * step
        put(s * step, step, dot3([r[:, :k] for r in left_refs], [r[rows, :k] for r in right_refs]))


def second_block(mine, theirs, big, core):
    width = big.shape[0]
    half = width // 2
    plane, group = mine.shape[:2]

    def kernel(core_ref, mine_ref, theirs_ref, inv_ref, sh_ref, sl_ref, ih_ref, il_ref, g, gl):
        ih_ref[...], il_ref[...] = two(jnp.where(lax.broadcasted_iota(jnp.int32, (width, width), 0) >= lax.broadcasted_iota(jnp.int32, (width, width), 1), inv_ref[...], 0.0))
        left = core_ref[0] == 0
        for zy in range(plane):
            for xc in range(group):
                at = (xc // 2 % 2) * half + zy * (width // 32) + (xc // 4) * 16 + (xc % 2) * 8
                u, v = mine_ref[zy, xc], theirs_ref[zy, xc]
                g[at:at + 8, :half] = jnp.where(left, u, v)
                g[at:at + 8, half:] = jnp.where(left, v, u)
        gl[0], gl[1] = two(g[...])

        def put(at, size, value):
            sh_ref[:, at:at + size], sl_ref[:, at:at + size] = two(value)

        lower_dot3([gl.at[0], gl.at[1]], [ih_ref, il_ref], put)

    out = jax.ShapeDtypeStruct((width, width), jnp.bfloat16)
    return pl.pallas_call(
        kernel,
        out_shape=(out,) * 4,
        in_specs=[SCALARS] + [WHOLE] * 3,
        out_specs=(WHOLE,) * 4,
        scratch_shapes=[pltpu.VMEM((width, width), jnp.float32), pltpu.VMEM((2, width, width), jnp.bfloat16)],
        compiler_params=params(50), name="second_block")(core, mine, theirs, big)


def finish(rows, cols, diag, second, inverse, prior, tm_index):
    quarter, cycles, frames = rows[0].shape
    width = cols.shape[1]
    count = quarter * cycles
    scale = 1.0 / (RING * frames)

    def kernel(tm_ref, r0, r1, r2, r3, cols_ref, diag_ref, sh_ref, sl_ref, ih_ref, il_ref, prior_hbm, panel_hbm, next_hbm, rows_v, acc, gh, gl, prior_v, sems, row_sems):
        k = pl.program_id(0)
        fetch = pltpu.make_async_copy(prior_hbm, prior_v, sems.at[0])

        @pl.when(k == 0)
        def _():
            for i, r in enumerate((r0, r1, r2, r3)):
                pltpu.make_async_copy(r, rows_v.at[i], row_sems.at[i]).start()
            fetch.start()

        pltpu.make_async_copy(r0, rows_v.at[k], row_sems.at[k]).wait()
        part = lax.dot_general(rows_v[k].reshape(count, frames), cols_ref[0], NT, preferred_element_type=jnp.float32)

        @pl.when(k == 0)
        def _():
            acc[...] = part.reshape(acc.shape)

        @pl.when(k > 0)
        def _():
            acc[...] += part.reshape(acc.shape)

        @pl.when(k == RING - 1)
        def _():
            cycle = lax.broadcasted_iota(jnp.int32, (1, cycles, width), 1)
            gram = acc[...] * scale + jnp.where(cycle == 0, diag_ref[...], 0.0)
            gh[...], gl[...] = two(gram.reshape(count, width))

            def put(at, size, value):
                acc[:, :, at:at + size] = value.reshape(quarter, cycles, size)

            lower_dot3([gh, gl], [ih_ref, il_ref], put)
            send_panel = pltpu.make_async_copy(acc, panel_hbm, sems.at[1])
            send_panel.start()
            gh[...], gl[...] = two(acc[...].reshape(count, width))
            fetch.wait()
            step = width // STRIPS
            for s in range(STRIPS):
                cut = pl.ds(s * step, step)
                update = dot3([gh[...], gl[...]], [sh_ref[cut, :], sl_ref[cut, :]])
                prior_v[:, :, s * step:(s + 1) * step] = prior_v[:, :, s * step:(s + 1) * step] - update.reshape(quarter, cycles, step)
            send_next = pltpu.make_async_copy(prior_v, next_hbm, sems.at[2])
            send_next.start()
            send_panel.wait()
            send_next.wait()

    whole2 = pl.BlockSpec((width, width), lambda i, tm: (0, 0), pipeline_mode=pl.Buffered(1))
    anywhere = pl.BlockSpec(memory_space=pl.ANY)
    out = jax.ShapeDtypeStruct((quarter, cycles, width), jnp.float32)
    return pl.pallas_call(
        kernel,
        out_shape=(out, out),
        grid_spec=pltpu.PrefetchScalarGridSpec(
            num_scalar_prefetch=1, grid=(RING,),
            in_specs=[anywhere] * RING + [pl.BlockSpec((1, width, frames), lambda i, tm: (jnp.bitwise_xor(tm[0], i), 0, 0)),
                      pl.BlockSpec((quarter, 1, width), lambda i, tm: (0, 0, 0))] + [whole2] * 4 + [anywhere],
            out_specs=(anywhere, anywhere),
            scratch_shapes=[pltpu.VMEM((RING, quarter, cycles, frames), jnp.bfloat16), pltpu.VMEM((quarter, cycles, width), jnp.float32)]
            + [pltpu.VMEM((count, width), jnp.bfloat16)] * 2
            + [pltpu.VMEM((quarter, cycles, width), jnp.float32), pltpu.SemaphoreType.DMA((3,)), pltpu.SemaphoreType.DMA((RING,))]),
        compiler_params=params(50), name="finish")(tm_index, *rows, cols, diag, *second, *inverse, prior)


def device_id(x, y, z, core):
    return ((x // 2) * 2 + core) * 32 + (x % 2) * 16 + z * 4 + y


DEVICES = [(x, y, z, c) for x in range(RING) for y in range(RING) for z in range(RING) for c in range(2)]


def send(value, step):
    return lax.ppermute(value, AXES, [(device_id(*d), device_id(*step(*d))) for d in DEVICES])


def swap_cores(value):
    return send(value, lambda x, y, z, c: (x, y, z, 1 - c))


def around(value, step):
    return [value] + [send(value, step(d)) for d in range(1, RING)]


def x_ring(d):
    return lambda x, y, z, c: ((x + d) % RING, y, z, c)


def inner_ring(d):
    return lambda x, y, z, c: (x, (y + d * (1 - c)) % RING, (z + d * c) % RING, c)


def outer_ring(d):
    return lambda x, y, z, c: (x, (y + d * c) % RING, (z + d * (1 - c)) % RING, c)


def flip_tm(k):
    return lambda x, y, z, c: (x ^ (k & 2), y, z, c ^ (k & 1))


CHIP_ROWS = [[device_id(x, y, z, c) for x in range(RING) for c in range(2)] for z in range(RING) for y in range(RING)]
PLANES = [[device_id(x, y, z, c) for z in range(RING) for y in range(RING)] for x in range(RING) for c in range(2)]


def shards(telemetry, frame_ids, valid, noise, prior_next):
    slope_index = lax.axis_index("slope")
    tm_index = lax.axis_index("tm")
    tel = telemetry[0]
    row_block, cycles, frames = tel.shape
    width = noise.shape[0]
    tm_count = 4
    quarter = row_block // tm_count
    core_index = tm_index % 2
    core = core_index.reshape(1)
    place = jnp.stack([core_index, (tm_index // 2) * 2 + slope_index // 16, slope_index % 4, (slope_index // 4) % 4])
    keep = lax.dynamic_slice(valid.reshape(cycles, 4), (0, slope_index // 8), (cycles, 1)).astype(jnp.float32)
    mine, theirs, second_own, hot = pick_first(tel, frame_ids[None, :], keep, core)
    pair = jnp.stack([mine, swap_cores(theirs)])
    by_x = jnp.stack(around(pair, x_ring))
    by_inner = jnp.stack(around(by_x, inner_ring))
    by_inner, hot, second_own = lax.optimization_barrier((by_inner, hot, second_own))
    own = around(by_inner, outer_ring)
    second_rows = lax.all_to_all(second_own.reshape(tm_count, quarter, frames), "tm", 0, 0)
    selected = pick_all(tel, hot, keep, tm_index.reshape(1))
    other = [swap_cores(piece) for piece in own]
    selected, own, other = lax.optimization_barrier((selected, own, other))
    rows = [selected[0], None, send(selected[2], flip_tm(2)), None]
    first_cols, lead, second_gram = lead_gram(own, other, second_rows, noise[None, :], place)
    near = lax.all_to_all(second_gram, AXES, 0, 0, axis_index_groups=CHIP_ROWS)
    big = chol_step(lead, 0, SPLIT[0])
    near, big, selected = lax.optimization_barrier((near, big, selected))
    rows[3] = send(selected[3], flip_tm(3))
    rows[1] = send(selected[1], flip_tm(1))
    near = lax.dynamic_slice_in_dim(near, core_index * (width // 2), width // 2, axis=2)
    near = jnp.broadcast_to(near[None], (16,) + near.shape)
    mine2 = lax.all_to_all(near, AXES, 0, 0, axis_index_groups=PLANES)
    big = chol_step(big, SPLIT[0], SPLIT[1])
    mine2, big = lax.optimization_barrier((mine2, big))
    theirs2 = swap_cores(mine2)
    big = chol_step(big, SPLIT[0] + SPLIT[1], SPLIT[2])
    split = second_block(mine2, theirs2, big, core)
    diag_ids = slope_index * row_block + tm_index * quarter + lax.broadcasted_iota(jnp.int32, (quarter, 1, width), 0)
    diag = jnp.where(diag_ids == lax.broadcasted_iota(jnp.int32, (quarter, 1, width), 2), noise[None, None, :], 0.0)
    panel, next_block = finish(rows, first_cols, diag, split[:2], split[2:], prior_next[0], tm_index.reshape(1))
    return panel[None], next_block[None]


def solution(mesh):
    return jax.shard_map(
        shards,
        mesh=mesh,
        in_specs=(P("slope", None, None, "tm"), P("tm"), P(), P(), P("slope", "tm", None, None)),
        out_specs=(P("slope", "tm", None, None), P("slope", "tm", None, None)),
        check_vma=False,
    )
```

time: 1060 us -> 257 us (0.24)
  waiting for transfers between devices: 568 us -> 82.3 us
  other arithmetic: 275 us -> 0.43 us
  Pallas kernels: 0 us -> 109 us
  matrix products: 90.1 us -> 0 us
  local copies, waits for them, and re-layouts: 89 us -> 25.4 us
  starting transfers between devices: 0.16 us -> 37 us
  between operations: 19.7 us -> 1.06 us
  blocking collectives: 15 us -> 0 us
    all_gather x3 -> x0, waiting for transfers between devices: 461 us -> none  [the longest x1 155 us: shards(): first_cols = lax.all_gather(selected[:, 0, :], 'slope', axis=0, tiled=True)]
    another operation x33 -> x4, other arithmetic: 257 us -> 0.27 us  [the longest x2 0.18 us: shards(): by_inner = jnp.stack(around(by_x, inner_ring))]
    pallas_call x0 -> x8, Pallas kernels: none -> 109 us  [the longest x3 46.9 us: chol_step(): pl.pallas_call(kernel, out_shape=jax.ShapeDtypeStruct(big.shape, jnp.floa...]
    reduce_scatter x1 -> x0, waiting for transfers between devices: 107 us -> none  [shards(): lax.psum_scatter(jnp.einsum('rcf,jf->rcj', selected, first_cols, preferre...]
    ppermute x0 -> x18, waiting for transfers between devices: none -> 80.6 us  [send(): lax.ppermute(value, AXES, [(device_id(*d), device_id(*step(*d))) for d in...]
    another operation x29 -> x0, matrix products: 46.2 us -> none  [the longest x15 23.1 us: shards(): jax.scipy.linalg.solve_triangular(factor, jnp.eye(block_width, dtype=jnp....]
    dot_general x3 -> x0, matrix products: 43.9 us -> none  [the longest x1 17.1 us: shards(): jnp.einsum('rci,ji->rcj', panel_rows, second, precision=lax.Precision.HIG...]
    another operation x33 -> x0, local copies, waits for them, and re-layouts: 29.8 us -> none
  transfers between devices with their start and end apart: 4 -> 21, of which waited for: 4 -> 10; matrix products, arithmetic and copies ran while one was open for 1% -> 0% of each run, Pallas kernels for 0% -> 27%
where the time goes in v1:
time: 257 us; the launch traced here: 255 us
  Pallas kernels  109 us (42%)
  waiting for transfers between devices  82.3 us (32%)
  starting transfers between devices  37 us (14%)
  local copies, waits for them, and re-layouts  25.4 us (10%)
    ppermute x18, waiting for transfers between devices, send(): lax.ppermute(value, AXES, [(device_id(*d), device_id(*step(*d))) for d in...  80.6 us
    pallas_call x3, Pallas kernels, chol_step(): pl.pallas_call(kernel, out_shape=jax.ShapeDtypeStruct(big.shape, jnp.floa...  46.9 us
    unnamed x32, local copies, waits for them, and re-layouts  23.1 us
    pallas_call x1, Pallas kernels, finish(): pl.pallas_call(kernel, out_shape=(out, out), grid_spec=pltpu.PrefetchScal...  22.9 us
    ppermute x18, starting transfers between devices, send(): lax.ppermute(value, AXES, [(device_id(*d), device_id(*step(*d))) for d in...  22.5 us
    pallas_call x1, Pallas kernels, lead_gram(): pl.pallas_call(kernel, out_shape=(jax.ShapeDtypeStruct((tm_count, width,...  15.5 us
    pallas_call x1, Pallas kernels, pick_all(): pl.pallas_call(kernel, out_shape=(jax.ShapeDtypeStruct((quarter, cycles,...  11.2 us
    pallas_call x1, Pallas kernels, second_block(): pl.pallas_call(kernel, out_shape=(out,) * 4, in_specs=[SCALARS] + [WHOLE]...  10.6 us
  transfers between devices with their start and end apart: 21, of which 10 were waited for; matrix products, arithmetic and copies ran while one was open for 0% of the time, Pallas kernels for 27%

profile of v1, /device:TPU:0, one launch (start us, length us, event | category | flops | bytes accessed | tf_op | source)
XLA Modules:
  0.0 255.2 jit_solution(10013436280499227920)
XLA Ops:
  1.5 2.8 %copy-done.7 = bf16[1,32,96,1024]{3,2,1,0:T(8,128)(2,1)S(1)} copy-done((bf16[1,32,96,1024]{3,2,1,0:T(8,128)(2,1)S(1)}, bf16[1,32,96,1024]{3,2,1,0:T(8,128)(2,1)}, u32[]{:S(2)}) %copy-start.7) | copy-done | bytes 6291480
  5.0 2.0 pick_first.1
  9.9 2.7 %collective-permute-start.2 = (bf16[2,16,1024]{2,1,0:T(8,128)(2,1)S(1)}, bf16[2,16,1024]{2,1,0:T(8,128)(2,1)S(1)}, u32[]{:S(2)}, u32[]{:S(2)}) collective-permute-start(bf16[2,16,1024]{2,1,0:T(8,128)(2,1)S(1)} %get-tuple-element.81), channel_id=1, source_target_pairs={{0,64},{32,96},{4,68},{36,100},{8,72},{40,104},{12,76},{44,108},{1... | collective-permute-start | bytes 196616 | tf_op jit(solution)/shard_map/ppermute | solution.py:399
  14.1 2.1 collective-permute-done.2
  18.6 2.9 %collective-permute-start.5 = (bf16[4,2,16,1024]{3,2,1,0:T(8,128)(2,1)S(1)}, bf16[4,2,16,1024]{3,2,1,0:T(8,128)(2,1)S(1)}, u32[]{:S(2)}, u32[]{:S(2)}) collective-permute-start(bf16[4,2,16,1024]{3,2,1,0:T(8,128)(2,1)S(1)} %get-tuple-element.79), channel_id=1, source_target_pairs={{0,2},{32,40},{4,6},{36,44},{8,10},{40,32},{12,14},{44,36},{1,3},{... | collective-permute-start | bytes 786440 | tf_op jit(solution)/shard_map/ppermute | solution.py:399
  22.8 1.8 collective-permute-done.4
  24.6 4.0 %collective-permute-done.5 = bf16[4,2,16,1024]{3,2,1,0:T(8,128)(2,1)S(1)} collective-permute-done((bf16[4,2,16,1024]{3,2,1,0:T(8,128)(2,1)S(1)}, bf16[4,2,16,1024]{3,2,1,0:T(8,128)(2,1)S(1)}, u32[]{:S(2)}, u32[]{:S(2)}) %collective-permute-start.5) | collective-permute-done | bytes 262176 | tf_op jit(solution)/shard_map/ppermute | solution.py:399
  28.8 2.0 collective-permute-start.7
  30.8 3.6 %collective-permute-start.8 = (bf16[4,4,2,16,1024]{4,3,2,1,0:T(8,128)(2,1)S(1)}, bf16[4,4,2,16,1024]{4,3,2,1,0:T(8,128)(2,1)}, u32[]{:S(2)}, u32[]{:S(2)}) collective-permute-start(bf16[4,4,2,16,1024]{4,3,2,1,0:T(8,128)(2,1)S(1)} %pad_maximum_fusion.refs_0_), channel_id=1, source_target_pairs={{0,8},{32,34},{4,12},{36,38},{8,0},{40,42},{12,4},{44,46},{1,9},{3... | collective-permute-start | bytes 3145736 | tf_op jit(solution)/shard_map/ppermute | solution.py:399
  35.4 10.4 %collective-permute-done.7.refs_1_ = bf16[4,4,2,16,1024]{4,3,2,1,0:T(8,128)(2,1)} collective-permute-done((bf16[4,4,2,16,1024]{4,3,2,1,0:T(8,128)(2,1)S(1)}, bf16[4,4,2,16,1024]{4,3,2,1,0:T(8,128)(2,1)}, u32[]{:S(2)}, u32[]{:S(2)}) %collective-permute-start.7) | collective-permute-done | bytes 1048608 | tf_op jit(solution)/shard_map/ppermute | solution.py:399
  45.8 12.7 %collective-permute-done.8.refs_2_ = bf16[4,4,2,16,1024]{4,3,2,1,0:T(8,128)(2,1)} collective-permute-done((bf16[4,4,2,16,1024]{4,3,2,1,0:T(8,128)(2,1)S(1)}, bf16[4,4,2,16,1024]{4,3,2,1,0:T(8,128)(2,1)}, u32[]{:S(2)}, u32[]{:S(2)}) %collective-permute-start.8) | collective-permute-done | bytes 1048608 | tf_op jit(solution)/shard_map/ppermute | solution.py:399
  59.0 3.3 %all-to-all-start = ((bf16[4,8,1024]{2,1,0:T(8,128)(2,1)}), bf16[4,8,1024]{2,1,0:T(8,128)(2,1)S(1)}, u32[]{:S(2)}, u32[]{:S(2)}) async-start(bf16[4,8,1024]{2,1,0:T(8,128)(2,1)} %bitcast.17), calls=%async_computation | async-start | bytes 131072 | tf_op jit(solution)/shard_map/all_to_all | solution.py:448
  62.4 11.2 %pick_all.1 = (bf16[8,96,1024]{2,1,0:T(8,128)(2,1)S(1)}, bf16[8,96,1024]{2,1,0:T(8,128)(2,1)S(1)}, bf16[8,96,1024]{2,1,0:T(8,128)(2,1)}, bf16[8,96,1024]{2,1,0:T(8,128)(2,1)S(1)}) custom-call(s32[1]{0:T(128)} %bitcast.tm_ref, bf16[32,96,1024]{2,1,0:T(8,128)(2,1)} %bitcast.24, bf16[1024,1024]{1,0:T(8,128)(2,1)S(1)} %get-tuple-element.44.hot_ref, ...), custom_call_target="tpu_custom_call" | custom-call | tf_op jit(solution)/shard_map/pick_all/pallas_call | solution.py:179
  77.1 15.5 %lead_gram.1 = (bf16[4,1024,1024]{2,1,0:T(8,128)(2,1)}, f32[1024,1024]{1,0:T(8,128)S(1)}, f32[8,8,1024]{2,1,0:T(8,128)}) custom-call(s32[4]{0:T(128)S(1)} %pad_add_fusion.place_ref, bf16[4,4,2,16,1024]{4,3,2,1,0:T(8,128)(2,1)S(1)} %pad_maximum_fusion.refs_0_, bf16[4,4,2,16,1024]{4,3,2,1,0:T(8,128)(2,1)} %collective-permute-done.7.refs_1_, ...), custom_call_target="tpu_custom_call" | custom-call | tf_op jit(solution)/shard_map/lead_gram/pallas_call | solution.py:260
  92.7 2.0 copy-done
  94.7 5.4 %all-to-all-start.1 = ((f32[8,8,1024]{2,1,0:T(8,128)}), f32[8,8,1024]{2,1,0:T(8,128)S(1)}, u32[]{:S(2)}, u32[]{:S(2)}) async-start(f32[8,8,1024]{2,1,0:T(8,128)} %get-tuple-element.60), calls=%async_computation.1 | async-start | bytes 524288 | tf_op jit(solution)/shard_map/all_to_all | solution.py:454
  100.1 2.2 copy-done.1
  102.3 14.3 %chol_panels.3.src = f32[1024,1024]{1,0:T(8,128)S(1)} custom-call(f32[1024,1024]{1,0:T(8,128)S(1)} %copy-done.1), custom_call_target="tpu_custom_call", output_to_operand_aliasing={{}: (0, {})} | custom-call | tf_op jit(solution)/shard_map/chol_panels/pallas_call | solution.py:127
  116.6 2.0 copy-done.2
  120.3 5.8 %all-to-all-start.2 = ((f32[16,8,8,512]{3,2,1,0:T(8,128)}), f32[16,8,8,512]{3,2,1,0:T(8,128)}, u32[]{:S(2)}, u32[]{:S(2)}) async-start(f32[16,8,8,512]{3,2,1,0:T(8,128)} %broadcast_in_dim.35), calls=%async_computation.2 | async-start | bytes 4194304 | tf_op jit(solution)/shard_map/all_to_all | solution.py:461
  126.1 2.2 copy-done.3
  128.3 28.3 %chol_panels.4.src = f32[1024,1024]{1,0:T(8,128)S(1)} custom-call(f32[1024,1024]{1,0:T(8,128)S(1)} %copy-done.3), custom_call_target="tpu_custom_call", output_to_operand_aliasing={{}: (0, {})} | custom-call | tf_op jit(solution)/shard_map/chol_panels/pallas_call | solution.py:127
  156.6 2.0 copy-done.4
  158.6 1.7 all-to-all-done.2.mine_ref
  160.3 2.2 collective-permute-start.15
  164.0 2.2 copy-done.5
  166.2 4.3 %chol_panels.5.inv_ref = f32[1024,1024]{1,0:T(8,128)S(1)} custom-call(f32[1024,1024]{1,0:T(8,128)S(1)} %copy-done.5), custom_call_target="tpu_custom_call", output_to_operand_aliasing={{}: (0, {})} | custom-call | tf_op jit(solution)/shard_map/chol_panels/pallas_call | solution.py:127
  170.6 2.0 copy-done.6
  172.6 10.6 %second_block.1 = (bf16[1024,1024]{1,0:T(8,128)(2,1)S(1)}, bf16[1024,1024]{1,0:T(8,128)(2,1)}, bf16[1024,1024]{1,0:T(8,128)(2,1)}, bf16[1024,1024]{1,0:T(8,128)(2,1)}) custom-call(s32[1]{0:T(128)} %bitcast.2.core_ref, f32[16,8,8,512]{3,2,1,0:T(8,128)} %all-to-all-done.2.mine_ref, f32[16,8,8,512]{3,2,1,0:T(8,128)} %collective-permute-done.17.theirs_ref, ...), custom_call_target="tpu_custom_call" | custom-call | tf_op jit(solution)/shard_map/second_block/pallas_call | solution.py:314
  184.5 14.9 %collective-permute-done.15.r2 = bf16[8,96,1024]{2,1,0:T(8,128)(2,1)} collective-permute-done((bf16[8,96,1024]{2,1,0:T(8,128)(2,1)}, bf16[8,96,1024]{2,1,0:T(8,128)(2,1)}, u32[]{:S(2)}, u32[]{:S(2)}) %collective-permute-start.15) | collective-permute-done | bytes 1572896 | tf_op jit(solution)/shard_map/ppermute | solution.py:399
  199.4 32.8 %collective-permute-done.16.r3 = bf16[8,96,1024]{2,1,0:T(8,128)(2,1)} collective-permute-done((bf16[8,96,1024]{2,1,0:T(8,128)(2,1)S(1)}, bf16[8,96,1024]{2,1,0:T(8,128)(2,1)}, u32[]{:S(2)}, u32[]{:S(2)}) %collective-permute-start.16) | collective-permute-done | bytes 1572896 | tf_op jit(solution)/shard_map/ppermute | solution.py:399
  232.2 22.9 %finish.1 = (f32[8,96,1024]{2,1,0:T(8,128)}, f32[8,96,1024]{2,1,0:T(8,128)}) custom-call(s32[1]{0:T(128)} %bitcast.tm_ref, bf16[8,96,1024]{2,1,0:T(8,128)(2,1)S(1)} %copy-done.10, bf16[8,96,1024]{2,1,0:T(8,128)(2,1)S(1)} %collective-permute-done.14.r1, bf16[8,96,1024]{2,1,0:T(8,128)(2,1)} %collective-permute-done.15.r2, ...), custom_call_target="tpu_custom_call" | custom-call | tf_op jit(solution)/shard_map/finish/pallas_call | solution.py:377
  (60 shorter events, 19.4 us)
Async XLA Ops:
  1.5 2.8 %copy-start.7 = (bf16[1,32,96,1024]{3,2,1,0:T(8,128)(2,1)S(1)}, bf16[1,32,96,1024]{3,2,1,0:T(8,128)(2,1)}, u32[]{:S(2)}) copy-start(bf16[1,32,96,1024]{3,2,1,0:T(8,128)(2,1)} %param.5) | copy-start | bytes 18874372
  7.0 1.2 collective-permute-start
  8.2 5.8 %collective-permute-start.1 = (bf16[2,16,1024]{2,1,0:T(8,128)(2,1)S(1)}, bf16[2,16,1024]{2,1,0:T(8,128)(2,1)S(1)}, u32[]{:S(2)}, u32[]{:S(2)}) collective-permute-start(bf16[2,16,1024]{2,1,0:T(8,128)(2,1)S(1)} %get-tuple-element.81), channel_id=1, source_target_pairs={{0,16},{32,48},{4,20},{36,52},{8,24},{40,56},{12,28},{44,60},{1,17... | collective-permute-start | bytes 196616 | tf_op jit(solution)/shard_map/ppermute | solution.py:399
  9.9 6.3 %collective-permute-start.2 = (bf16[2,16,1024]{2,1,0:T(8,128)(2,1)S(1)}, bf16[2,16,1024]{2,1,0:T(8,128)(2,1)S(1)}, u32[]{:S(2)}, u32[]{:S(2)}) collective-permute-start(bf16[2,16,1024]{2,1,0:T(8,128)(2,1)S(1)} %get-tuple-element.81), channel_id=1, source_target_pairs={{0,64},{32,96},{4,68},{36,100},{8,72},{40,104},{12,76},{44,108},{1... | collective-permute-start | bytes 196616 | tf_op jit(solution)/shard_map/ppermute | solution.py:399
  12.6 4.3 %collective-permute-start.3 = (bf16[2,16,1024]{2,1,0:T(8,128)(2,1)S(1)}, bf16[2,16,1024]{2,1,0:T(8,128)(2,1)S(1)}, u32[]{:S(2)}, u32[]{:S(2)}) collective-permute-start(bf16[2,16,1024]{2,1,0:T(8,128)(2,1)S(1)} %get-tuple-element.81), channel_id=1, source_target_pairs={{0,80},{32,112},{4,84},{36,116},{8,88},{40,120},{12,92},{44,124},{... | collective-permute-start | bytes 196616 | tf_op jit(solution)/shard_map/ppermute | solution.py:399
  16.9 7.7 %collective-permute-start.4 = (bf16[4,2,16,1024]{3,2,1,0:T(8,128)(2,1)S(1)}, bf16[4,2,16,1024]{3,2,1,0:T(8,128)(2,1)S(1)}, u32[]{:S(2)}, u32[]{:S(2)}) collective-permute-start(bf16[4,2,16,1024]{3,2,1,0:T(8,128)(2,1)S(1)} %get-tuple-element.79), channel_id=1, source_target_pairs={{0,1},{32,36},{4,5},{36,40},{8,9},{40,44},{12,13},{44,32},{1,2},{3... | collective-permute-start | bytes 786440 | tf_op jit(solution)/shard_map/ppermute | solution.py:399
  18.6 10.1 %collective-permute-start.5 = (bf16[4,2,16,1024]{3,2,1,0:T(8,128)(2,1)S(1)}, bf16[4,2,16,1024]{3,2,1,0:T(8,128)(2,1)S(1)}, u32[]{:S(2)}, u32[]{:S(2)}) collective-permute-start(bf16[4,2,16,1024]{3,2,1,0:T(8,128)(2,1)S(1)} %get-tuple-element.79), channel_id=1, source_target_pairs={{0,2},{32,40},{4,6},{36,44},{8,10},{40,32},{12,14},{44,36},{1,3},{... | collective-permute-start | bytes 786440 | tf_op jit(solution)/shard_map/ppermute | solution.py:399
  21.5 7.2 %collective-permute-start.6 = (bf16[4,2,16,1024]{3,2,1,0:T(8,128)(2,1)S(1)}, bf16[4,2,16,1024]{3,2,1,0:T(8,128)(2,1)S(1)}, u32[]{:S(2)}, u32[]{:S(2)}) collective-permute-start(bf16[4,2,16,1024]{3,2,1,0:T(8,128)(2,1)S(1)} %get-tuple-element.79), channel_id=1, source_target_pairs={{0,3},{32,44},{4,7},{36,32},{8,11},{40,36},{12,15},{44,40},{1,0},{... | collective-permute-start | bytes 786440 | tf_op jit(solution)/shard_map/ppermute | solution.py:399
  28.8 17.0 %collective-permute-start.7 = (bf16[4,4,2,16,1024]{4,3,2,1,0:T(8,128)(2,1)S(1)}, bf16[4,4,2,16,1024]{4,3,2,1,0:T(8,128)(2,1)}, u32[]{:S(2)}, u32[]{:S(2)}) collective-permute-start(bf16[4,4,2,16,1024]{4,3,2,1,0:T(8,128)(2,1)S(1)} %pad_maximum_fusion.refs_0_), channel_id=1, source_target_pairs={{0,4},{32,33},{4,8},{36,37},{8,12},{40,41},{12,0},{44,45},{1,5},{3... | collective-permute-start | bytes 3145736 | tf_op jit(solution)/shard_map/ppermute | solution.py:399
  30.8 27.7 %collective-permute-start.8 = (bf16[4,4,2,16,1024]{4,3,2,1,0:T(8,128)(2,1)S(1)}, bf16[4,4,2,16,1024]{4,3,2,1,0:T(8,128)(2,1)}, u32[]{:S(2)}, u32[]{:S(2)}) collective-permute-start(bf16[4,4,2,16,1024]{4,3,2,1,0:T(8,128)(2,1)S(1)} %pad_maximum_fusion.refs_0_), channel_id=1, source_target_pairs={{0,8},{32,34},{4,12},{36,38},{8,0},{40,42},{12,4},{44,46},{1,9},{3... | collective-permute-start | bytes 3145736 | tf_op jit(solution)/shard_map/ppermute | solution.py:399
  34.4 24.1 %collective-permute-start.9 = (bf16[4,4,2,16,1024]{4,3,2,1,0:T(8,128)(2,1)S(1)}, bf16[4,4,2,16,1024]{4,3,2,1,0:T(8,128)(2,1)}, u32[]{:S(2)}, u32[]{:S(2)}) collective-permute-start(bf16[4,4,2,16,1024]{4,3,2,1,0:T(8,128)(2,1)S(1)} %pad_maximum_fusion.refs_0_), channel_id=1, source_target_pairs={{0,12},{32,35},{4,0},{36,39},{8,4},{40,43},{12,8},{44,47},{1,13},{... | collective-permute-start | bytes 3145736 | tf_op jit(solution)/shard_map/ppermute | solution.py:399
  35.4 41.7 %collective-permute-start.10 = (bf16[4,4,2,16,1024]{4,3,2,1,0:T(8,128)(2,1)S(1)}, bf16[4,4,2,16,1024]{4,3,2,1,0:T(8,128)(2,1)}, u32[]{:S(2)}, u32[]{:S(2)}) collective-permute-start(bf16[4,4,2,16,1024]{4,3,2,1,0:T(8,128)(2,1)S(1)} %pad_maximum_fusion.refs_0_), channel_id=1, source_target_pairs={{0,32},{32,0},{4,36},{36,4},{8,40},{40,8},{12,44},{44,12},{1,33},{... | collective-permute-start | bytes 3145736 | tf_op jit(solution)/shard_map/ppermute | solution.py:399
  45.8 31.3 %collective-permute-start.11 = (bf16[4,4,2,16,1024]{4,3,2,1,0:T(8,128)(2,1)}, bf16[4,4,2,16,1024]{4,3,2,1,0:T(8,128)(2,1)}, u32[]{:S(2)}, u32[]{:S(2)}) collective-permute-start(bf16[4,4,2,16,1024]{4,3,2,1,0:T(8,128)(2,1)} %collective-permute-done.7.refs_1_), channel_id=1, source_target_pairs={{0,32},{32,0},{4,36},{36,4},{8,40},{40,8},{12,44},{44,12},{1,33},{... | collective-permute-start | bytes 3145736 | tf_op jit(solution)/shard_map/ppermute | solution.py:399
  58.5 18.6 %collective-permute-start.12 = (bf16[4,4,2,16,1024]{4,3,2,1,0:T(8,128)(2,1)}, bf16[4,4,2,16,1024]{4,3,2,1,0:T(8,128)(2,1)}, u32[]{:S(2)}, u32[]{:S(2)}) collective-permute-start(bf16[4,4,2,16,1024]{4,3,2,1,0:T(8,128)(2,1)} %collective-permute-done.8.refs_2_), channel_id=1, source_target_pairs={{0,32},{32,0},{4,36},{36,4},{8,40},{40,8},{12,44},{44,12},{1,33},{... | collective-permute-start | bytes 3145736 | tf_op jit(solution)/shard_map/ppermute | solution.py:399
  58.5 18.6 %collective-permute-start.13 = (bf16[4,4,2,16,1024]{4,3,2,1,0:T(8,128)(2,1)}, bf16[4,4,2,16,1024]{4,3,2,1,0:T(8,128)(2,1)}, u32[]{:S(2)}, u32[]{:S(2)}) collective-permute-start(bf16[4,4,2,16,1024]{4,3,2,1,0:T(8,128)(2,1)} %collective-permute-done.9.refs_3_), channel_id=1, source_target_pairs={{0,32},{32,0},{4,36},{36,4},{8,40},{40,8},{12,44},{44,12},{1,33},{... | collective-permute-start | bytes 3145736 | tf_op jit(solution)/shard_map/ppermute | solution.py:399
  59.0 18.1 %all-to-all-start = ((bf16[4,8,1024]{2,1,0:T(8,128)(2,1)}), bf16[4,8,1024]{2,1,0:T(8,128)(2,1)S(1)}, u32[]{:S(2)}, u32[]{:S(2)}) async-start(bf16[4,8,1024]{2,1,0:T(8,128)(2,1)} %bitcast.17), calls=%async_computation | async-start | bytes 131072 | tf_op jit(solution)/shard_map/all_to_all | solution.py:448
  62.4 14.8 %copy-start.11 = (f32[1024]{0:T(1024)S(1)}, f32[1024]{0:T(1024)}, u32[]{:S(2)}) copy-start(f32[1024]{0:T(1024)} %param.8) | copy-start | bytes 12292
  92.7 2.0 copy-start
  94.7 24.0 %all-to-all-start.1 = ((f32[8,8,1024]{2,1,0:T(8,128)}), f32[8,8,1024]{2,1,0:T(8,128)S(1)}, u32[]{:S(2)}, u32[]{:S(2)}) async-start(f32[8,8,1024]{2,1,0:T(8,128)} %get-tuple-element.60), calls=%async_computation.1 | async-start | bytes 524288 | tf_op jit(solution)/shard_map/all_to_all | solution.py:454
  100.1 2.2 copy-start.1
  116.6 2.0 copy-start.2
  120.3 40.0 %all-to-all-start.2 = ((f32[16,8,8,512]{3,2,1,0:T(8,128)}), f32[16,8,8,512]{3,2,1,0:T(8,128)}, u32[]{:S(2)}, u32[]{:S(2)}) async-start(f32[16,8,8,512]{3,2,1,0:T(8,128)} %broadcast_in_dim.35), calls=%async_computation.2 | async-start | bytes 4194304 | tf_op jit(solution)/shard_map/all_to_all | solution.py:461
  126.1 2.2 copy-start.3
  128.3 34.4 %copy-start.14 = (bf16[8,96,1024]{2,1,0:T(8,128)(2,1)S(1)}, bf16[8,96,1024]{2,1,0:T(8,128)(2,1)}, u32[]{:S(2)}) copy-start(bf16[8,96,1024]{2,1,0:T(8,128)(2,1)} %copy-done.13) | copy-start | bytes 4718596
  156.6 2.0 copy-start.4
  160.3 12.3 %collective-permute-start.17 = (f32[16,8,8,512]{3,2,1,0:T(8,128)}, f32[16,8,8,512]{3,2,1,0:T(8,128)}, u32[]{:S(2)}, u32[]{:S(2)}) collective-permute-start(f32[16,8,8,512]{3,2,1,0:T(8,128)} %all-to-all-done.2.mine_ref), channel_id=1, source_target_pairs={{0,32},{32,0},{4,36},{36,4},{8,40},{40,8},{12,44},{44,12},{1,33},{... | collective-permute-start | bytes 6291464 | tf_op jit(solution)/shard_map/ppermute | solution.py:399
  160.3 39.1 %collective-permute-start.15 = (bf16[8,96,1024]{2,1,0:T(8,128)(2,1)}, bf16[8,96,1024]{2,1,0:T(8,128)(2,1)}, u32[]{:S(2)}, u32[]{:S(2)}) collective-permute-start(bf16[8,96,1024]{2,1,0:T(8,128)(2,1)} %get-tuple-element.63), channel_id=1, source_target_pairs={{0,64},{32,96},{4,68},{36,100},{8,72},{40,104},{12,76},{44,108},{1... | collective-permute-start | bytes 4718600 | tf_op jit(solution)/shard_map/ppermute | solution.py:399
  162.5 36.9 %collective-permute-start.14 = (bf16[8,96,1024]{2,1,0:T(8,128)(2,1)}, bf16[8,96,1024]{2,1,0:T(8,128)(2,1)S(1)}, u32[]{:S(2)}, u32[]{:S(2)}) collective-permute-start(bf16[8,96,1024]{2,1,0:T(8,128)(2,1)} %copy-done.15), channel_id=1, source_target_pairs={{0,32},{32,0},{4,36},{36,4},{8,40},{40,8},{12,44},{44,12},{1,33},{... | collective-permute-start | bytes 4718600 | tf_op jit(solution)/shard_map/ppermute | solution.py:399
  162.7 69.4 %collective-permute-start.16 = (bf16[8,96,1024]{2,1,0:T(8,128)(2,1)S(1)}, bf16[8,96,1024]{2,1,0:T(8,128)(2,1)}, u32[]{:S(2)}, u32[]{:S(2)}) collective-permute-start(bf16[8,96,1024]{2,1,0:T(8,128)(2,1)S(1)} %copy-done.14), channel_id=1, source_target_pairs={{0,96},{32,64},{4,100},{36,68},{8,104},{40,72},{12,108},{44,76},{1... | collective-permute-start | bytes 4718600 | tf_op jit(solution)/shard_map/ppermute | solution.py:399
  164.0 2.2 copy-start.5
  170.6 2.0 copy-start.6
  172.6 59.5 %copy-start.10 = (bf16[8,96,1024]{2,1,0:T(8,128)(2,1)S(1)}, bf16[8,96,1024]{2,1,0:T(8,128)(2,1)}, u32[]{:S(2)}) copy-start(bf16[8,96,1024]{2,1,0:T(8,128)(2,1)} %copy-done.9) | copy-start | bytes 4718596
  (5 other events, 5.6 us)

commit v2 on v1

--- a/solution.py
+++ b/solution.py
@@ -10,6 +10,10 @@
 TN = (((0,), (0,)), ((), ()))
 NT = (((1,), (1,)), ((), ()))
 WHOLE = pl.BlockSpec(memory_space=pltpu.VMEM)
+
+
+def in_hbm(value):
+    return pltpu.with_memory_space_constraint(value, pltpu.HBM)
 
 
 def params(mib=40):
@@ -78,12 +82,26 @@
             a, x = na, nx
 
 
-def chol_panels(first, count, big, wa, wx, linv, ys):
+def chol_panels(first, count, src, dst, big, wa, wx, linv, ys, arrive, leave):
     n = big.shape[0]
     nblk = n // NB
+    last = first + count - 1
     rows = lax.broadcasted_iota(jnp.int32, (NB, NB), 0)
     lanes = lax.broadcasted_iota(jnp.int32, (NB, NB), 1)
     eye = jnp.where(rows == lanes, 1.0, 0.0)
+
+    def block(i):
+        return pl.ds(pl.multiple_of(i * NB, NB), NB)
+
+    def load(i):
+        return pltpu.make_async_copy(src.at[block(i)], big.at[block(i)], arrive.at[i])
+
+    def store(i):
+        return pltpu.make_async_copy(big.at[block(i)], dst.at[block(i)], leave.at[i])
+
+    for i in range(first, nblk):
+        load(i).start()
+    load(first).wait()
 
     def panel_step(p, carry):
         at = pl.multiple_of(p * NB, NB)
@@ -93,12 +111,18 @@
         factor_block(wa, wx, linv)
         y = jnp.dot(linv[...], big[pl.ds(at, NB), :], precision=lax.Precision.HIGHEST, preferred_element_type=jnp.float32)
         big[pl.ds(at, NB), :] = y
+        store(p).start()
         high, mid, low = (part.astype(jnp.bfloat16) for part in split3(y))
         for i, part in enumerate((high, mid, low, high)):
             ys[i * NB:(i + 1) * NB, :] = part
 
         def trail(i, c):
             row = pl.multiple_of(i * NB, NB)
+
+            @pl.when(p == first)
+            def _():
+                load(i).wait()
+
             big[pl.ds(row, NB), pl.ds(at, NB)] = jnp.zeros((NB, NB), jnp.float32)
             hm = ys[0:2 * NB, pl.ds(row, NB)]
             mh = jnp.concatenate([ys[NB:2 * NB, pl.ds(row, NB)], ys[0:NB, pl.ds(row, NB)]], axis=0)
@@ -107,41 +131,55 @@
             dot = lambda u, v: lax.dot_general(u, v, TN, preferred_element_type=jnp.float32)
             upd = dot(hm, ys[0:2 * NB, :]) + (dot(mh, ys[0:2 * NB, :]) + dot(lh, hl))
             big[pl.ds(row, NB), :] = big[pl.ds(row, NB), :] - upd
+
+            @pl.when(p == last)
+            def _():
+                store(i).start()
+
             return c
 
         lax.fori_loop(p + 1, nblk, trail, 0)
         return carry
 
-    lax.fori_loop(first, first + count, panel_step, 0)
+    lax.fori_loop(first, last + 1, panel_step, 0)
+    for i in range(first, nblk):
+        store(i).wait()
 
 
 CHOL_SCRATCH = [pltpu.VMEM((NB, NB), jnp.float32)] * 3
 
 
-def chol_step(big, first, count):
-    n = big.shape[0]
-
-    def kernel(src, dst, wa, wx, linv, ys):
-        chol_panels(first, count, dst, wa, wx, linv, ys)
-
+def chol_step(src, first, count):
+    n = src.shape[0]
+    blocks = n // NB
+
+    def kernel(src_ref, dst_ref, big, wa, wx, linv, ys, arrive, leave):
+        chol_panels(first, count, src_ref, dst_ref, big, wa, wx, linv, ys, arrive, leave)
+
+    hbm = pl.BlockSpec(memory_space=pltpu.HBM)
     return pl.pallas_call(
-        kernel, out_shape=jax.ShapeDtypeStruct(big.shape, jnp.float32), in_specs=[WHOLE], out_specs=WHOLE,
-        scratch_shapes=CHOL_SCRATCH + [pltpu.VMEM((4 * NB, n), jnp.bfloat16)], input_output_aliases={0: 0},
-        compiler_params=params(), name="chol_panels")(big)
+        kernel, out_shape=pltpu.HBM((n, n), jnp.float32), in_specs=[hbm], out_specs=hbm,
+        scratch_shapes=[pltpu.VMEM((n, n), jnp.float32)] + CHOL_SCRATCH
+        + [pltpu.VMEM((4 * NB, n), jnp.bfloat16), pltpu.SemaphoreType.DMA((blocks,)), pltpu.SemaphoreType.DMA((blocks,))],
+        input_output_aliases={0: 0}, compiler_params=params(24), name="chol_panels")(in_hbm(src))
 
 
 SPLIT = (2, 5, 1)
 AXES = ("tm", "slope")
 RING = 4
 SCALARS = pl.BlockSpec(memory_space=pltpu.SMEM)
+HBM = pl.BlockSpec(memory_space=pltpu.HBM)
 
 
 def pick_first(tel, ids, keep, core):
     rows, _, frames = tel.shape
     half = rows // 2
 
-    def kernel(core_ref, tel_ref, ids_ref, keep_ref, mine_ref, theirs_ref, second_ref, hot_ref, got, lead):
+    def kernel(core_ref, tel_hbm, ids_ref, keep_ref, mine_ref, theirs_ref, second_ref, hot_ref, got, lead, tel_ref, sem):
+        fetch = pltpu.make_async_copy(tel_hbm.at[:, pl.ds(0, 16), :], tel_ref, sem)
+        fetch.start()
         hot_ref[...] = jnp.where(lax.broadcasted_iota(jnp.int32, (frames, frames), 0) == ids_ref[...], 1.0, 0.0).astype(jnp.bfloat16)
+        fetch.wait()
         got[...] = jnp.dot(tel_ref[...].reshape(rows * 16, frames), hot_ref[...], preferred_element_type=jnp.float32).reshape(rows, 16, frames)
         lead[...] = got[:, 0, :] * keep_ref[0:1, 0:1]
         at = pl.multiple_of(core_ref[0] * half, half)
@@ -155,10 +193,11 @@
         kernel,
         grid=(1,),
         out_shape=tuple(jax.ShapeDtypeStruct(s, jnp.bfloat16) for s in shapes),
-        in_specs=[SCALARS, pl.BlockSpec((rows, 16, frames), lambda i: (0, 0, 0)), whole((1, frames)), whole(keep.shape)],
+        in_specs=[SCALARS, HBM, whole((1, frames)), whole(keep.shape)],
         out_specs=tuple(whole(s) for s in shapes),
-        scratch_shapes=[pltpu.VMEM((rows, 16, frames), jnp.float32), pltpu.VMEM((rows, frames), jnp.float32)],
-        compiler_params=params(), name="pick_first")(core, tel, ids, keep)
+        scratch_shapes=[pltpu.VMEM((rows, 16, frames), jnp.float32), pltpu.VMEM((rows, frames), jnp.float32),
+                        pltpu.VMEM((rows, 16, frames), tel.dtype), pltpu.SemaphoreType.DMA],
+        compiler_params=params(), name="pick_first")(core, in_hbm(tel), ids, keep)
 
 
 def pick_all(tel, hot, keep, tm_index):
@@ -177,13 +216,13 @@
 
     place = lambda k: pl.BlockSpec((per, cycles, frames), lambda i, tm: (jnp.clip(i - steps * k, 0, steps - 1), 0, 0))
     return pl.pallas_call(
-        kernel, out_shape=(jax.ShapeDtypeStruct((quarter, cycles, frames), jnp.bfloat16),) * RING,
+        kernel, out_shape=(pltpu.HBM((quarter, cycles, frames), jnp.bfloat16),) * RING,
         grid_spec=pltpu.PrefetchScalarGridSpec(
             num_scalar_prefetch=1, grid=(rows // per,),
             in_specs=[pl.BlockSpec((per, cycles, frames), lambda i, tm: (jnp.bitwise_xor(tm[0], i // steps) * steps + i % steps, 0, 0)),
                       pl.BlockSpec((frames, frames), lambda i, tm: (0, 0)), pl.BlockSpec(keep.shape, lambda i, tm: (0, 0))],
             out_specs=tuple(place(k) for k in range(RING))),
-        compiler_params=params(), name="pick_all")(tm_index, tel, hot, keep)
+        compiler_params=params(), name="pick_all")(tm_index, in_hbm(tel), hot, keep)
 
 
 def lead_gram(own, other, second_rows, noise, place):
@@ -195,7 +234,7 @@
 
     def kernel(place_ref, *refs):
         parts = (refs[:RING], refs[RING:2 * RING])
-        rows_ref, noise_ref, cols_hbm, gram_ref, second_ref, left, acc, arrive, leave = refs[2 * RING:]
+        rows_ref, noise_ref, cols_hbm, gram_hbm, second_ref, left, acc, arrive, leave, gram_sem = refs[2 * RING:]
         me_core, me_x, me_y, me_z = (place_ref[i] for i in range(4))
 
         def fetch(t, slot):
@@ -247,24 +286,27 @@
             return carry
 
         lax.fori_loop(0, tm_count, one, 0)
-        rows = lax.broadcasted_iota(jnp.int32, (width, width), 0)
-        diag = rows == lax.broadcasted_iota(jnp.int32, (width, width), 1)
-        gram_ref[...] = acc[:width, :] * scale + jnp.where(diag, noise_ref[...], 0.0)
+        rows = lax.broadcasted_iota(jnp.int32, (NB, width), 0)
+        cols = lax.broadcasted_iota(jnp.int32, (NB, width), 1)
+        for at in range(0, width, NB):
+            acc[at:at + NB, :] = acc[at:at + NB, :] * scale + jnp.where(rows + at == cols, noise_ref[...], 0.0)
+            pltpu.make_async_copy(acc.at[pl.ds(at, NB)], gram_hbm.at[pl.ds(at, NB)], gram_sem).start()
         second = acc[width:width + quarter, :] * scale
         for i in range(group):
             second_ref[i] = second
+        pltpu.make_async_copy(acc.at[pl.ds(0, width)], gram_hbm, gram_sem).wait()
         out_copy(tm_count - 2, 0).wait()
         out_copy(tm_count - 1, 1).wait()
 
     anywhere = pl.BlockSpec(memory_space=pl.ANY)
     return pl.pallas_call(
         kernel,
-        out_shape=(jax.ShapeDtypeStruct((tm_count, width, frames), jnp.bfloat16), jax.ShapeDtypeStruct((width, width), jnp.float32),
+        out_shape=(pltpu.HBM((tm_count, width, frames), jnp.bfloat16), pltpu.HBM((width, width), jnp.float32),
                    jax.ShapeDtypeStruct((group, quarter, width), jnp.float32)),
         in_specs=[SCALARS] + [anywhere] * (2 * RING) + [WHOLE] * 2,
-        out_specs=(anywhere, WHOLE, WHOLE),
+        out_specs=(HBM, HBM, WHOLE),
         scratch_shapes=[pltpu.VMEM((2, width + 16, frames), jnp.bfloat16), pltpu.VMEM((width + 16, width), jnp.float32),
-                        pltpu.SemaphoreType.DMA((2,)), pltpu.SemaphoreType.DMA((2,))],
+                        pltpu.SemaphoreType.DMA((2,)), pltpu.SemaphoreType.DMA((2,)), pltpu.SemaphoreType.DMA],
         compiler_params=params(40), name="lead_gram")(place, *own, *other, second_rows, noise)
 
 
@@ -289,52 +331,29 @@
         put(s * step, step, dot3([r[:, :k] for r in left_refs], [r[rows, :k] for r in right_refs]))
 
 
-def second_block(mine, theirs, big, core):
-    width = big.shape[0]
+def finish(rows, cols, diag, mine, theirs, inverse, prior, tm_index):
+    quarter, cycles, frames = rows[0].shape
+    width = cols.shape[1]
     half = width // 2
     plane, group = mine.shape[:2]
-
-    def kernel(core_ref, mine_ref, theirs_ref, inv_ref, sh_ref, sl_ref, ih_ref, il_ref, g, gl):
-        ih_ref[...], il_ref[...] = two(jnp.where(lax.broadcasted_iota(jnp.int32, (width, width), 0) >= lax.broadcasted_iota(jnp.int32, (width, width), 1), inv_ref[...], 0.0))
-        left = core_ref[0] == 0
-        for zy in range(plane):
-            for xc in range(group):
-                at = (xc // 2 % 2) * half + zy * (width // 32) + (xc // 4) * 16 + (xc % 2) * 8
-                u, v = mine_ref[zy, xc], theirs_ref[zy, xc]
-                g[at:at + 8, :half] = jnp.where(left, u, v)
-                g[at:at + 8, half:] = jnp.where(left, v, u)
-        gl[0], gl[1] = two(g[...])
-
-        def put(at, size, value):
-            sh_ref[:, at:at + size], sl_ref[:, at:at + size] = two(value)
-
-        lower_dot3([gl.at[0], gl.at[1]], [ih_ref, il_ref], put)
-
-    out = jax.ShapeDtypeStruct((width, width), jnp.bfloat16)
-    return pl.pallas_call(
-        kernel,
-        out_shape=(out,) * 4,
-        in_specs=[SCALARS] + [WHOLE] * 3,
-        out_specs=(WHOLE,) * 4,
-        scratch_shapes=[pltpu.VMEM((width, width), jnp.float32), pltpu.VMEM((2, width, width), jnp.bfloat16)],
-        compiler_params=params(50), name="second_block")(core, mine, theirs, big)
-
-
-def finish(rows, cols, diag, second, inverse, prior, tm_index):
-    quarter, cycles, frames = rows[0].shape
-    width = cols.shape[1]
     count = quarter * cycles
     scale = 1.0 / (RING * frames)
 
-    def kernel(tm_ref, r0, r1, r2, r3, cols_ref, diag_ref, sh_ref, sl_ref, ih_ref, il_ref, prior_hbm, panel_hbm, next_hbm, rows_v, acc, gh, gl, prior_v, sems, row_sems):
+    def kernel(tm_ref, r0, r1, r2, r3, cols_ref, diag_ref, mine_hbm, theirs_hbm, inv_hbm, prior_hbm, panel_hbm, next_hbm,
+               rows_v, acc, gh, gl, prior_v, pieces, inv_v, ih, il, g, sh, sl, sems, row_sems):
         k = pl.program_id(0)
-        fetch = pltpu.make_async_copy(prior_hbm, prior_v, sems.at[0])
+        left = tm_ref[0] % 2 == 0
+        fetches = [
+            pltpu.make_async_copy(inv_hbm, inv_v, sems.at[0]), pltpu.make_async_copy(mine_hbm, pieces.at[0], sems.at[1]),
+            pltpu.make_async_copy(theirs_hbm, pieces.at[1], sems.at[2]), pltpu.make_async_copy(prior_hbm, prior_v, sems.at[3]),
+        ]
 
         @pl.when(k == 0)
         def _():
             for i, r in enumerate((r0, r1, r2, r3)):
                 pltpu.make_async_copy(r, rows_v.at[i], row_sems.at[i]).start()
-            fetch.start()
+            for f in fetches:
+                f.start()
 
         pltpu.make_async_copy(r0, rows_v.at[k], row_sems.at[k]).wait()
         part = lax.dot_general(rows_v[k].reshape(count, frames), cols_ref[0], NT, preferred_element_type=jnp.float32)
@@ -349,6 +368,10 @@
 
         @pl.when(k == RING - 1)
         def _():
+            for f in fetches:
+                f.wait()
+            tril = lax.broadcasted_iota(jnp.int32, (width, width), 0) >= lax.broadcasted_iota(jnp.int32, (width, width), 1)
+            ih[...], il[...] = two(jnp.where(tril, inv_v[...], 0.0))
             cycle = lax.broadcasted_iota(jnp.int32, (1, cycles, width), 1)
             gram = acc[...] * scale + jnp.where(cycle == 0, diag_ref[...], 0.0)
             gh[...], gl[...] = two(gram.reshape(count, width))
@@ -356,36 +379,52 @@
             def put(at, size, value):
                 acc[:, :, at:at + size] = value.reshape(quarter, cycles, size)
 
-            lower_dot3([gh, gl], [ih_ref, il_ref], put)
-            send_panel = pltpu.make_async_copy(acc, panel_hbm, sems.at[1])
+            lower_dot3([gh, gl], [ih, il], put)
+            send_panel = pltpu.make_async_copy(acc, panel_hbm, sems.at[4])
             send_panel.start()
+
+            def place(zy, carry):
+                for xc in range(group):
+                    at = pl.multiple_of((xc // 2 % 2) * half + zy * (width // 32) + (xc // 4) * 16 + (xc % 2) * 8, 8)
+                    u, v = pieces[0, zy, xc], pieces[1, zy, xc]
+                    inv_v[pl.ds(at, 8), :half] = jnp.where(left, u, v)
+                    inv_v[pl.ds(at, 8), half:] = jnp.where(left, v, u)
+                return carry
+
+            lax.fori_loop(0, plane, place, 0)
+            g[0], g[1] = two(inv_v[...])
+
+            def put_second(at, size, value):
+                sh[:, at:at + size], sl[:, at:at + size] = two(value)
+
+            lower_dot3([g.at[0], g.at[1]], [ih, il], put_second)
             gh[...], gl[...] = two(acc[...].reshape(count, width))
-            fetch.wait()
             step = width // STRIPS
             for s in range(STRIPS):
                 cut = pl.ds(s * step, step)
-                update = dot3([gh[...], gl[...]], [sh_ref[cut, :], sl_ref[cut, :]])
+                update = dot3([gh[...], gl[...]], [sh[cut, :], sl[cut, :]])
                 prior_v[:, :, s * step:(s + 1) * step] = prior_v[:, :, s * step:(s + 1) * step] - update.reshape(quarter, cycles, step)
-            send_next = pltpu.make_async_copy(prior_v, next_hbm, sems.at[2])
+            send_next = pltpu.make_async_copy(prior_v, next_hbm, sems.at[5])
             send_next.start()
             send_panel.wait()
             send_next.wait()
 
-    whole2 = pl.BlockSpec((width, width), lambda i, tm: (0, 0), pipeline_mode=pl.Buffered(1))
-    anywhere = pl.BlockSpec(memory_space=pl.ANY)
     out = jax.ShapeDtypeStruct((quarter, cycles, width), jnp.float32)
+    square = pltpu.VMEM((width, width), jnp.bfloat16)
     return pl.pallas_call(
         kernel,
         out_shape=(out, out),
         grid_spec=pltpu.PrefetchScalarGridSpec(
             num_scalar_prefetch=1, grid=(RING,),
-            in_specs=[anywhere] * RING + [pl.BlockSpec((1, width, frames), lambda i, tm: (jnp.bitwise_xor(tm[0], i), 0, 0)),
-                      pl.BlockSpec((quarter, 1, width), lambda i, tm: (0, 0, 0))] + [whole2] * 4 + [anywhere],
-            out_specs=(anywhere, anywhere),
+            in_specs=[HBM] * RING + [pl.BlockSpec((1, width, frames), lambda i, tm: (jnp.bitwise_xor(tm[0], i), 0, 0)),
+                      pl.BlockSpec((quarter, 1, width), lambda i, tm: (0, 0, 0))] + [HBM] * 4,
+            out_specs=(HBM, HBM),
             scratch_shapes=[pltpu.VMEM((RING, quarter, cycles, frames), jnp.bfloat16), pltpu.VMEM((quarter, cycles, width), jnp.float32)]
             + [pltpu.VMEM((count, width), jnp.bfloat16)] * 2
-            + [pltpu.VMEM((quarter, cycles, width), jnp.float32), pltpu.SemaphoreType.DMA((3,)), pltpu.SemaphoreType.DMA((RING,))]),
-        compiler_params=params(50), name="finish")(tm_index, *rows, cols, diag, *second, *inverse, prior)
+            + [pltpu.VMEM((quarter, cycles, width), jnp.float32), pltpu.VMEM((2,) + mine.shape, jnp.float32), pltpu.VMEM((width, width), jnp.float32)]
+            + [square] * 2 + [pltpu.VMEM((2, width, width), jnp.bfloat16)] + [square] * 2
+            + [pltpu.SemaphoreType.DMA((6,)), pltpu.SemaphoreType.DMA((RING,))]),
+        compiler_params=params(56), name="finish")(tm_index, *map(in_hbm, rows), cols, diag, in_hbm(mine), in_hbm(theirs), in_hbm(inverse), in_hbm(prior))
 
 
 def device_id(x, y, z, core):
@@ -463,10 +502,9 @@
     mine2, big = lax.optimization_barrier((mine2, big))
     theirs2 = swap_cores(mine2)
     big = chol_step(big, SPLIT[0] + SPLIT[1], SPLIT[2])
-    split = second_block(mine2, theirs2, big, core)
     diag_ids = slope_index * row_block + tm_index * quarter + lax.broadcasted_iota(jnp.int32, (quarter, 1, width), 0)
     diag = jnp.where(diag_ids == lax.broadcasted_iota(jnp.int32, (quarter, 1, width), 2), noise[None, None, :], 0.0)
-    panel, next_block = finish(rows, first_cols, diag, split[:2], split[2:], prior_next[0], tm_index.reshape(1))
+    panel, next_block = finish(rows, first_cols, diag, mine2, theirs2, big, prior_next[0], tm_index.reshape(1))
     return panel[None], next_block[None]
 
 

time: 257 us -> 257 us (level)
  local copies, waits for them, and re-layouts: 25.4 us -> 3.06 us
  waiting for transfers between devices: 82.3 us -> 98.7 us
  Pallas kernels: 109 us -> 115 us
    unnamed x32 -> x6, local copies, waits for them, and re-layouts: 23.1 us -> 0.69 us
    ppermute x18, waiting for transfers between devices: 80.6 us -> 94.7 us  [send(): lax.ppermute(value, AXES, [(device_id(*d), device_id(*step(*d))) for d in...]
    pallas_call x1, Pallas kernels: 22.9 us -> 29 us  [finish(): pl.pallas_call(kernel, out_shape=(out, out), grid_spec=pltpu.PrefetchScal...]
    pallas_call x6 -> x5, Pallas kernels: 84.1 us -> 82.7 us  [the longest x3 52.8 us: chol_step(): pl.pallas_call(kernel, out_shape=pltpu.HBM((n, n), jnp.float32), in_specs...]
  transfers between devices with their start and end apart: 21 -> 21, of which waited for: 10 -> 10; matrix products, arithmetic and copies ran while one was open for 0% -> 0% of each run, Pallas kernels for 27% -> 26%
where the time goes in v2:
time: 257 us; the launch traced here: 255 us
  Pallas kernels  115 us (45%)
  waiting for transfers between devices  98.7 us (38%)
  starting transfers between devices  36.8 us (14%)
  local copies, waits for them, and re-layouts  3.06 us (1%)
    ppermute x18, waiting for transfers between devices, send(): lax.ppermute(value, AXES, [(device_id(*d), device_id(*step(*d))) for d in...  94.7 us
    pallas_call x3, Pallas kernels, chol_step(): pl.pallas_call(kernel, out_shape=pltpu.HBM((n, n), jnp.float32), in_specs...  52.8 us
    pallas_call x1, Pallas kernels, finish(): pl.pallas_call(kernel, out_shape=(out, out), grid_spec=pltpu.PrefetchScal...  29 us
    ppermute x18, starting transfers between devices, send(): lax.ppermute(value, AXES, [(device_id(*d), device_id(*step(*d))) for d in...  22.7 us
    pallas_call x1, Pallas kernels, lead_gram(): pl.pallas_call(kernel, out_shape=(pltpu.HBM((tm_count, width, frames), jn...  17.3 us
    pallas_call x1, Pallas kernels, pick_all(): pl.pallas_call(kernel, out_shape=(pltpu.HBM((quarter, cycles, frames), jn...  12.6 us
    all_to_all x1, starting transfers between devices, shards(): near = lax.all_to_all(second_gram, AXES, 0, 0, axis_index_groups=CHIP_ROWS)  6.39 us
  transfers between devices with their start and end apart: 21, of which 10 were waited for; matrix products, arithmetic and copies ran while one was open for 0% of the time, Pallas kernels for 26%

profile of v2, /device:TPU:0, one launch (start us, length us, event | category | flops | bytes accessed | tf_op | source)
XLA Modules:
  0.0 255.5 jit_solution(14945891863866184950)
XLA Ops:
  0.7 0.8 reshape.68
  1.5 0.7 copy-done.1
  2.2 3.2 %pick_first.1 = (bf16[16,1024]{1,0:T(8,128)(2,1)S(1)}, bf16[16,1024]{1,0:T(8,128)(2,1)S(1)}, bf16[32,1024]{1,0:T(8,128)(2,1)}, bf16[1024,1024]{1,0:T(8,128)(2,1)S(1)}) custom-call(s32[1]{0:T(128)} %bitcast.2.core_ref, bf16[32,96,1024]{2,1,0:T(8,128)(2,1)} %bitcast.27, s32[1,1024]{1,0:T(1,128)S(1)} %bitcast.26, f32[96,1]{1,0:T(8,128)S(1)} %dynamic-slice_convert_fusion.keep_ref), custom_call_target="tpu_custom_call" | custom-call | tf_op jit(solution)/shard_map/pick_first/pallas_call | solution.py:192
  5.5 1.2 collective-permute-done
  6.7 3.2 %collective-permute-start.2 = (bf16[2,16,1024]{2,1,0:T(8,128)(2,1)S(1)}, bf16[2,16,1024]{2,1,0:T(8,128)(2,1)S(1)}, u32[]{:S(2)}, u32[]{:S(2)}) collective-permute-start(bf16[2,16,1024]{2,1,0:T(8,128)(2,1)S(1)} %get-tuple-element.73), channel_id=1, source_target_pairs={{0,64},{32,96},{4,68},{36,100},{8,72},{40,104},{12,76},{44,108},{1... | collective-permute-start | bytes 196616 | tf_op jit(solution)/shard_map/ppermute | solution.py:438
  10.5 2.6 %collective-permute-start.3 = (bf16[2,16,1024]{2,1,0:T(8,128)(2,1)S(1)}, bf16[2,16,1024]{2,1,0:T(8,128)(2,1)S(1)}, u32[]{:S(2)}, u32[]{:S(2)}) collective-permute-start(bf16[2,16,1024]{2,1,0:T(8,128)(2,1)S(1)} %get-tuple-element.73), channel_id=1, source_target_pairs={{0,80},{32,112},{4,84},{36,116},{8,88},{40,120},{12,92},{44,124},{... | collective-permute-start | bytes 196616 | tf_op jit(solution)/shard_map/ppermute | solution.py:438
  13.2 2.2 collective-permute-done.1
  15.5 3.3 %collective-permute-start.5 = (bf16[4,2,16,1024]{3,2,1,0:T(8,128)(2,1)S(1)}, bf16[4,2,16,1024]{3,2,1,0:T(8,128)(2,1)S(1)}, u32[]{:S(2)}, u32[]{:S(2)}) collective-permute-start(bf16[4,2,16,1024]{3,2,1,0:T(8,128)(2,1)S(1)} %get-tuple-element.71), channel_id=1, source_target_pairs={{0,2},{32,40},{4,6},{36,44},{8,10},{40,32},{12,14},{44,36},{1,3},{... | collective-permute-start | bytes 786440 | tf_op jit(solution)/shard_map/ppermute | solution.py:438
  18.8 0.7 collective-permute-start.4
  19.4 2.6 %collective-permute-start.6 = (bf16[4,2,16,1024]{3,2,1,0:T(8,128)(2,1)S(1)}, bf16[4,2,16,1024]{3,2,1,0:T(8,128)(2,1)S(1)}, u32[]{:S(2)}, u32[]{:S(2)}) collective-permute-start(bf16[4,2,16,1024]{3,2,1,0:T(8,128)(2,1)S(1)} %get-tuple-element.71), channel_id=1, source_target_pairs={{0,3},{32,44},{4,7},{36,32},{8,11},{40,36},{12,15},{44,40},{1,0},{... | collective-permute-start | bytes 786440 | tf_op jit(solution)/shard_map/ppermute | solution.py:438
  22.0 1.4 collective-permute-done.5
  23.4 2.9 %collective-permute-done.4 = bf16[4,2,16,1024]{3,2,1,0:T(8,128)(2,1)S(1)} collective-permute-done((bf16[4,2,16,1024]{3,2,1,0:T(8,128)(2,1)S(1)}, bf16[4,2,16,1024]{3,2,1,0:T(8,128)(2,1)S(1)}, u32[]{:S(2)}, u32[]{:S(2)}) %collective-permute-start.4) | collective-permute-done | bytes 262176 | tf_op jit(solution)/shard_map/ppermute | solution.py:438
  26.7 4.1 %collective-permute-start.9 = (bf16[4,4,2,16,1024]{4,3,2,1,0:T(8,128)(2,1)S(1)}, bf16[4,4,2,16,1024]{4,3,2,1,0:T(8,128)(2,1)}, u32[]{:S(2)}, u32[]{:S(2)}) collective-permute-start(bf16[4,4,2,16,1024]{4,3,2,1,0:T(8,128)(2,1)S(1)} %pad_maximum_fusion.refs_0_), channel_id=1, source_target_pairs={{0,12},{32,35},{4,0},{36,39},{8,4},{40,43},{12,8},{44,47},{1,13},{... | collective-permute-start | bytes 3145736 | tf_op jit(solution)/shard_map/ppermute | solution.py:438
  30.9 1.3 collective-permute-start.7
  32.2 22.2 %collective-permute-done.9.refs_3_ = bf16[4,4,2,16,1024]{4,3,2,1,0:T(8,128)(2,1)} collective-permute-done((bf16[4,4,2,16,1024]{4,3,2,1,0:T(8,128)(2,1)S(1)}, bf16[4,4,2,16,1024]{4,3,2,1,0:T(8,128)(2,1)}, u32[]{:S(2)}, u32[]{:S(2)}) %collective-permute-start.9) | collective-permute-done | bytes 1048608 | tf_op jit(solution)/shard_map/ppermute | solution.py:438
  54.9 3.3 %collective-permute-done.7.refs_1_ = bf16[4,4,2,16,1024]{4,3,2,1,0:T(8,128)(2,1)} collective-permute-done((bf16[4,4,2,16,1024]{4,3,2,1,0:T(8,128)(2,1)S(1)}, bf16[4,4,2,16,1024]{4,3,2,1,0:T(8,128)(2,1)}, u32[]{:S(2)}, u32[]{:S(2)}) %collective-permute-start.7) | collective-permute-done | bytes 1048608 | tf_op jit(solution)/shard_map/ppermute | solution.py:438
  58.2 3.3 %all-to-all-start = ((bf16[4,8,1024]{2,1,0:T(8,128)(2,1)}), bf16[4,8,1024]{2,1,0:T(8,128)(2,1)S(1)}, u32[]{:S(2)}, u32[]{:S(2)}) async-start(bf16[4,8,1024]{2,1,0:T(8,128)(2,1)} %bitcast.17), calls=%async_computation | async-start | bytes 131072 | tf_op jit(solution)/shard_map/all_to_all | solution.py:487
  61.6 12.6 %pick_all.1 = (bf16[8,96,1024]{2,1,0:T(8,128)(2,1)}, bf16[8,96,1024]{2,1,0:T(8,128)(2,1)}, bf16[8,96,1024]{2,1,0:T(8,128)(2,1)}, bf16[8,96,1024]{2,1,0:T(8,128)(2,1)}) custom-call(s32[1]{0:T(128)} %bitcast.tm_ref, bf16[32,96,1024]{2,1,0:T(8,128)(2,1)} %bitcast.28, bf16[1024,1024]{1,0:T(8,128)(2,1)S(1)} %get-tuple-element.40.hot_ref, ...), custom_call_target="tpu_custom_call" | custom-call | tf_op jit(solution)/shard_map/pick_all/pallas_call | solution.py:218
  74.2 17.3 %lead_gram.1 = (bf16[4,1024,1024]{2,1,0:T(8,128)(2,1)}, f32[1024,1024]{1,0:T(8,128)}, f32[8,8,1024]{2,1,0:T(8,128)}) custom-call(s32[4]{0:T(128)S(1)} %pad_add_fusion.place_ref, bf16[4,4,2,16,1024]{4,3,2,1,0:T(8,128)(2,1)S(1)} %pad_maximum_fusion.refs_0_, bf16[4,4,2,16,1024]{4,3,2,1,0:T(8,128)(2,1)} %collective-permute-done.7.refs_1_, ...), custom_call_target="tpu_custom_call" | custom-call | tf_op jit(solution)/shard_map/lead_gram/pallas_call | solution.py:302
  91.5 6.4 %all-to-all-start.1 = ((f32[8,8,1024]{2,1,0:T(8,128)}), f32[8,8,1024]{2,1,0:T(8,128)S(1)}, u32[]{:S(2)}, u32[]{:S(2)}) async-start(f32[8,8,1024]{2,1,0:T(8,128)} %get-tuple-element.56), calls=%async_computation.1 | async-start | bytes 524288 | tf_op jit(solution)/shard_map/all_to_all | solution.py:493
  97.9 16.2 %chol_panels.3.src_ref = f32[1024,1024]{1,0:T(8,128)} custom-call(f32[1024,1024]{1,0:T(8,128)} %get-tuple-element.57.src_ref), custom_call_target="tpu_custom_call", output_to_operand_aliasing={{}: (0, {})} | custom-call | tf_op jit(solution)/shard_map/chol_panels/pallas_call | solution.py:160
  114.2 1.6 broadcast_in_dim.35
  115.8 4.4 %all-to-all-start.2 = ((f32[16,8,8,512]{3,2,1,0:T(8,128)}), f32[16,8,8,512]{3,2,1,0:T(8,128)S(1)}, u32[]{:S(2)}, u32[]{:S(2)}) async-start(f32[16,8,8,512]{3,2,1,0:T(8,128)} %broadcast_in_dim.35), calls=%async_computation.2 | async-start | bytes 4194304 | tf_op jit(solution)/shard_map/all_to_all | solution.py:500
  120.2 30.2 %chol_panels.4.src_ref = f32[1024,1024]{1,0:T(8,128)} custom-call(f32[1024,1024]{1,0:T(8,128)} %chol_panels.3.src_ref), custom_call_target="tpu_custom_call", output_to_operand_aliasing={{}: (0, {})} | custom-call | tf_op jit(solution)/shard_map/chol_panels/pallas_call | solution.py:160
  150.4 4.0 %all-to-all-done.2.mine_hbm = f32[16,8,8,512]{3,2,1,0:T(8,128)S(1)} async-done(((f32[16,8,8,512]{3,2,1,0:T(8,128)}), f32[16,8,8,512]{3,2,1,0:T(8,128)S(1)}, u32[]{:S(2)}, u32[]{:S(2)}) %all-to-all-start.2) | async-done | bytes 2097184 | tf_op jit(solution)/shard_map/all_to_all | solution.py:500
  154.4 2.2 collective-permute-start.15
  156.8 1.2 collective-permute-start.16
  158.1 0.7 compare_select_fusion.diag_ref
  158.8 6.4 %chol_panels.5.inv_hbm = f32[1024,1024]{1,0:T(8,128)} custom-call(f32[1024,1024]{1,0:T(8,128)} %chol_panels.4.src_ref), custom_call_target="tpu_custom_call", output_to_operand_aliasing={{}: (0, {})} | custom-call | tf_op jit(solution)/shard_map/chol_panels/pallas_call | solution.py:160
  165.1 28.4 %collective-permute-done.15.r2 = bf16[8,96,1024]{2,1,0:T(8,128)(2,1)} collective-permute-done((bf16[8,96,1024]{2,1,0:T(8,128)(2,1)}, bf16[8,96,1024]{2,1,0:T(8,128)(2,1)}, u32[]{:S(2)}, u32[]{:S(2)}) %collective-permute-start.15) | collective-permute-done | bytes 1572896 | tf_op jit(solution)/shard_map/ppermute | solution.py:438
  193.5 32.8 %collective-permute-done.16.r3 = bf16[8,96,1024]{2,1,0:T(8,128)(2,1)} collective-permute-done((bf16[8,96,1024]{2,1,0:T(8,128)(2,1)}, bf16[8,96,1024]{2,1,0:T(8,128)(2,1)}, u32[]{:S(2)}, u32[]{:S(2)}) %collective-permute-start.16) | collective-permute-done | bytes 1572896 | tf_op jit(solution)/shard_map/ppermute | solution.py:438
  226.3 29.0 %finish.1 = (f32[8,96,1024]{2,1,0:T(8,128)}, f32[8,96,1024]{2,1,0:T(8,128)}) custom-call(s32[1]{0:T(128)} %bitcast.tm_ref, bf16[8,96,1024]{2,1,0:T(8,128)(2,1)} %get-tuple-element.46.r0, bf16[8,96,1024]{2,1,0:T(8,128)(2,1)} %collective-permute-done.14.r1, bf16[8,96,1024]{2,1,0:T(8,128)(2,1)} %collective-permute-done.15.r2, ...), custom_call_target="tpu_custom_call" | custom-call | tf_op jit(solution)/shard_map/finish/pallas_call | solution.py:414
  (33 shorter events, 2.1 us)
Async XLA Ops:
  1.5 0.7 copy-start.1
  5.4 1.3 collective-permute-start
  6.7 6.5 %collective-permute-start.2 = (bf16[2,16,1024]{2,1,0:T(8,128)(2,1)S(1)}, bf16[2,16,1024]{2,1,0:T(8,128)(2,1)S(1)}, u32[]{:S(2)}, u32[]{:S(2)}) collective-permute-start(bf16[2,16,1024]{2,1,0:T(8,128)(2,1)S(1)} %get-tuple-element.73), channel_id=1, source_target_pairs={{0,64},{32,96},{4,68},{36,100},{8,72},{40,104},{12,76},{44,108},{1... | collective-permute-start | bytes 196616 | tf_op jit(solution)/shard_map/ppermute | solution.py:438
  9.9 5.5 %collective-permute-start.1 = (bf16[2,16,1024]{2,1,0:T(8,128)(2,1)S(1)}, bf16[2,16,1024]{2,1,0:T(8,128)(2,1)S(1)}, u32[]{:S(2)}, u32[]{:S(2)}) collective-permute-start(bf16[2,16,1024]{2,1,0:T(8,128)(2,1)S(1)} %get-tuple-element.73), channel_id=1, source_target_pairs={{0,16},{32,48},{4,20},{36,52},{8,24},{40,56},{12,28},{44,60},{1,17... | collective-permute-start | bytes 196616 | tf_op jit(solution)/shard_map/ppermute | solution.py:438
  10.5 4.9 %collective-permute-start.3 = (bf16[2,16,1024]{2,1,0:T(8,128)(2,1)S(1)}, bf16[2,16,1024]{2,1,0:T(8,128)(2,1)S(1)}, u32[]{:S(2)}, u32[]{:S(2)}) collective-permute-start(bf16[2,16,1024]{2,1,0:T(8,128)(2,1)S(1)} %get-tuple-element.73), channel_id=1, source_target_pairs={{0,80},{32,112},{4,84},{36,116},{8,88},{40,120},{12,92},{44,124},{... | collective-permute-start | bytes 196616 | tf_op jit(solution)/shard_map/ppermute | solution.py:438
  15.5 8.0 %collective-permute-start.5 = (bf16[4,2,16,1024]{3,2,1,0:T(8,128)(2,1)S(1)}, bf16[4,2,16,1024]{3,2,1,0:T(8,128)(2,1)S(1)}, u32[]{:S(2)}, u32[]{:S(2)}) collective-permute-start(bf16[4,2,16,1024]{3,2,1,0:T(8,128)(2,1)S(1)} %get-tuple-element.71), channel_id=1, source_target_pairs={{0,2},{32,40},{4,6},{36,44},{8,10},{40,32},{12,14},{44,36},{1,3},{... | collective-permute-start | bytes 786440 | tf_op jit(solution)/shard_map/ppermute | solution.py:438
  18.8 7.6 %collective-permute-start.4 = (bf16[4,2,16,1024]{3,2,1,0:T(8,128)(2,1)S(1)}, bf16[4,2,16,1024]{3,2,1,0:T(8,128)(2,1)S(1)}, u32[]{:S(2)}, u32[]{:S(2)}) collective-permute-start(bf16[4,2,16,1024]{3,2,1,0:T(8,128)(2,1)S(1)} %get-tuple-element.71), channel_id=1, source_target_pairs={{0,1},{32,36},{4,5},{36,40},{8,9},{40,44},{12,13},{44,32},{1,2},{3... | collective-permute-start | bytes 786440 | tf_op jit(solution)/shard_map/ppermute | solution.py:438
  19.4 7.2 %collective-permute-start.6 = (bf16[4,2,16,1024]{3,2,1,0:T(8,128)(2,1)S(1)}, bf16[4,2,16,1024]{3,2,1,0:T(8,128)(2,1)S(1)}, u32[]{:S(2)}, u32[]{:S(2)}) collective-permute-start(bf16[4,2,16,1024]{3,2,1,0:T(8,128)(2,1)S(1)} %get-tuple-element.71), channel_id=1, source_target_pairs={{0,3},{32,44},{4,7},{36,32},{8,11},{40,36},{12,15},{44,40},{1,0},{... | collective-permute-start | bytes 786440 | tf_op jit(solution)/shard_map/ppermute | solution.py:438
  26.7 27.7 %collective-permute-start.9 = (bf16[4,4,2,16,1024]{4,3,2,1,0:T(8,128)(2,1)S(1)}, bf16[4,4,2,16,1024]{4,3,2,1,0:T(8,128)(2,1)}, u32[]{:S(2)}, u32[]{:S(2)}) collective-permute-start(bf16[4,4,2,16,1024]{4,3,2,1,0:T(8,128)(2,1)S(1)} %pad_maximum_fusion.refs_0_), channel_id=1, source_target_pairs={{0,12},{32,35},{4,0},{36,39},{8,4},{40,43},{12,8},{44,47},{1,13},{... | collective-permute-start | bytes 3145736 | tf_op jit(solution)/shard_map/ppermute | solution.py:438
  30.8 23.6 %collective-permute-start.8 = (bf16[4,4,2,16,1024]{4,3,2,1,0:T(8,128)(2,1)S(1)}, bf16[4,4,2,16,1024]{4,3,2,1,0:T(8,128)(2,1)}, u32[]{:S(2)}, u32[]{:S(2)}) collective-permute-start(bf16[4,4,2,16,1024]{4,3,2,1,0:T(8,128)(2,1)S(1)} %pad_maximum_fusion.refs_0_), channel_id=1, source_target_pairs={{0,8},{32,34},{4,12},{36,38},{8,0},{40,42},{12,4},{44,46},{1,9},{3... | collective-permute-start | bytes 3145736 | tf_op jit(solution)/shard_map/ppermute | solution.py:438
  30.9 27.4 %collective-permute-start.7 = (bf16[4,4,2,16,1024]{4,3,2,1,0:T(8,128)(2,1)S(1)}, bf16[4,4,2,16,1024]{4,3,2,1,0:T(8,128)(2,1)}, u32[]{:S(2)}, u32[]{:S(2)}) collective-permute-start(bf16[4,4,2,16,1024]{4,3,2,1,0:T(8,128)(2,1)S(1)} %pad_maximum_fusion.refs_0_), channel_id=1, source_target_pairs={{0,4},{32,33},{4,8},{36,37},{8,12},{40,41},{12,0},{44,45},{1,5},{3... | collective-permute-start | bytes 3145736 | tf_op jit(solution)/shard_map/ppermute | solution.py:438
  32.2 42.0 %collective-permute-start.10 = (bf16[4,4,2,16,1024]{4,3,2,1,0:T(8,128)(2,1)S(1)}, bf16[4,4,2,16,1024]{4,3,2,1,0:T(8,128)(2,1)}, u32[]{:S(2)}, u32[]{:S(2)}) collective-permute-start(bf16[4,4,2,16,1024]{4,3,2,1,0:T(8,128)(2,1)S(1)} %pad_maximum_fusion.refs_0_), channel_id=1, source_target_pairs={{0,32},{32,0},{4,36},{36,4},{8,40},{40,8},{12,44},{44,12},{1,33},{... | collective-permute-start | bytes 3145736 | tf_op jit(solution)/shard_map/ppermute | solution.py:438
  54.4 19.8 %collective-permute-start.13 = (bf16[4,4,2,16,1024]{4,3,2,1,0:T(8,128)(2,1)}, bf16[4,4,2,16,1024]{4,3,2,1,0:T(8,128)(2,1)}, u32[]{:S(2)}, u32[]{:S(2)}) collective-permute-start(bf16[4,4,2,16,1024]{4,3,2,1,0:T(8,128)(2,1)} %collective-permute-done.9.refs_3_), channel_id=1, source_target_pairs={{0,32},{32,0},{4,36},{36,4},{8,40},{40,8},{12,44},{44,12},{1,33},{... | collective-permute-start | bytes 3145736 | tf_op jit(solution)/shard_map/ppermute | solution.py:438
  54.4 19.8 %collective-permute-start.12 = (bf16[4,4,2,16,1024]{4,3,2,1,0:T(8,128)(2,1)}, bf16[4,4,2,16,1024]{4,3,2,1,0:T(8,128)(2,1)}, u32[]{:S(2)}, u32[]{:S(2)}) collective-permute-start(bf16[4,4,2,16,1024]{4,3,2,1,0:T(8,128)(2,1)} %collective-permute-done.8.refs_2_), channel_id=1, source_target_pairs={{0,32},{32,0},{4,36},{36,4},{8,40},{40,8},{12,44},{44,12},{1,33},{... | collective-permute-start | bytes 3145736 | tf_op jit(solution)/shard_map/ppermute | solution.py:438
  58.2 16.0 %collective-permute-start.11 = (bf16[4,4,2,16,1024]{4,3,2,1,0:T(8,128)(2,1)}, bf16[4,4,2,16,1024]{4,3,2,1,0:T(8,128)(2,1)}, u32[]{:S(2)}, u32[]{:S(2)}) collective-permute-start(bf16[4,4,2,16,1024]{4,3,2,1,0:T(8,128)(2,1)} %collective-permute-done.7.refs_1_), channel_id=1, source_target_pairs={{0,32},{32,0},{4,36},{36,4},{8,40},{40,8},{12,44},{44,12},{1,33},{... | collective-permute-start | bytes 3145736 | tf_op jit(solution)/shard_map/ppermute | solution.py:438
  58.2 16.0 %all-to-all-start = ((bf16[4,8,1024]{2,1,0:T(8,128)(2,1)}), bf16[4,8,1024]{2,1,0:T(8,128)(2,1)S(1)}, u32[]{:S(2)}, u32[]{:S(2)}) async-start(bf16[4,8,1024]{2,1,0:T(8,128)(2,1)} %bitcast.17), calls=%async_computation | async-start | bytes 131072 | tf_op jit(solution)/shard_map/all_to_all | solution.py:487
  61.6 12.6 %copy-start = (f32[1024]{0:T(1024)S(1)}, f32[1024]{0:T(1024)}, u32[]{:S(2)}) copy-start(f32[1024]{0:T(1024)} %param.8) | copy-start | bytes 12292
  91.5 22.6 %all-to-all-start.1 = ((f32[8,8,1024]{2,1,0:T(8,128)}), f32[8,8,1024]{2,1,0:T(8,128)S(1)}, u32[]{:S(2)}, u32[]{:S(2)}) async-start(f32[8,8,1024]{2,1,0:T(8,128)} %get-tuple-element.56), calls=%async_computation.1 | async-start | bytes 524288 | tf_op jit(solution)/shard_map/all_to_all | solution.py:493
  115.8 38.6 %all-to-all-start.2 = ((f32[16,8,8,512]{3,2,1,0:T(8,128)}), f32[16,8,8,512]{3,2,1,0:T(8,128)S(1)}, u32[]{:S(2)}, u32[]{:S(2)}) async-start(f32[16,8,8,512]{3,2,1,0:T(8,128)} %broadcast_in_dim.35), calls=%async_computation.2 | async-start | bytes 4194304 | tf_op jit(solution)/shard_map/all_to_all | solution.py:500
  154.4 10.7 %copy-start.2 = (f32[16,8,8,512]{3,2,1,0:T(8,128)}, f32[16,8,8,512]{3,2,1,0:T(8,128)S(1)}, u32[]{:S(2)}) copy-start(f32[16,8,8,512]{3,2,1,0:T(8,128)S(1)} %all-to-all-done.2.mine_hbm) | copy-start | bytes 6291460
  154.4 71.9 %collective-permute-start.17 = (f32[16,8,8,512]{3,2,1,0:T(8,128)S(1)}, f32[16,8,8,512]{3,2,1,0:T(8,128)}, u32[]{:S(2)}, u32[]{:S(2)}) collective-permute-start(f32[16,8,8,512]{3,2,1,0:T(8,128)S(1)} %all-to-all-done.2.mine_hbm), channel_id=1, source_target_pairs={{0,32},{32,0},{4,36},{36,4},{8,40},{40,8},{12,44},{44,12},{1,33},{... | collective-permute-start | bytes 6291464 | tf_op jit(solution)/shard_map/ppermute | solution.py:438
  154.4 39.1 %collective-permute-start.15 = (bf16[8,96,1024]{2,1,0:T(8,128)(2,1)}, bf16[8,96,1024]{2,1,0:T(8,128)(2,1)}, u32[]{:S(2)}, u32[]{:S(2)}) collective-permute-start(bf16[8,96,1024]{2,1,0:T(8,128)(2,1)} %get-tuple-element.59), channel_id=1, source_target_pairs={{0,64},{32,96},{4,68},{36,100},{8,72},{40,104},{12,76},{44,108},{1... | collective-permute-start | bytes 4718600 | tf_op jit(solution)/shard_map/ppermute | solution.py:438
  156.6 36.9 %collective-permute-start.14 = (bf16[8,96,1024]{2,1,0:T(8,128)(2,1)}, bf16[8,96,1024]{2,1,0:T(8,128)(2,1)}, u32[]{:S(2)}, u32[]{:S(2)}) collective-permute-start(bf16[8,96,1024]{2,1,0:T(8,128)(2,1)} %get-tuple-element.61), channel_id=1, source_target_pairs={{0,32},{32,0},{4,36},{36,4},{8,40},{40,8},{12,44},{44,12},{1,33},{... | collective-permute-start | bytes 4718600 | tf_op jit(solution)/shard_map/ppermute | solution.py:438
  156.8 69.4 %collective-permute-start.16 = (bf16[8,96,1024]{2,1,0:T(8,128)(2,1)}, bf16[8,96,1024]{2,1,0:T(8,128)(2,1)}, u32[]{:S(2)}, u32[]{:S(2)}) collective-permute-start(bf16[8,96,1024]{2,1,0:T(8,128)(2,1)} %get-tuple-element.62), channel_id=1, source_target_pairs={{0,96},{32,64},{4,100},{36,68},{8,104},{40,72},{12,108},{44,76},{1... | collective-permute-start | bytes 4718600 | tf_op jit(solution)/shard_map/ppermute | solution.py:438

commit v3 on v2

--- a/solution.py
+++ b/solution.py
@@ -35,18 +35,22 @@
     return jnp.broadcast_to(z[j:j + 1, :], z.shape)
 
 
+AHEAD = 2
+
+
 def factor_block(wa, wx, out):
     sub = lax.broadcasted_iota(jnp.int32, (MB, NB), 0)
-    a = wa[0:MB, :]
-    x = wx[0:MB, :]
-    for k in range(NB // MB):
+    groups = NB // MB
+    rows_of = lambda k: (wa[k * MB:(k + 1) * MB, :], wx[k * MB:(k + 1) * MB, :])
+    window = [rows_of(k) for k in range(AHEAD)]
+    for k in range(groups):
         lo = MB * k
-        after = lo + MB < NB
-        cols = [jnp.broadcast_to(a[:, lo + j:lo + j + 1], (MB, NB)) for j in range(MB)]
-        if after:
-            na = wa[lo + MB:lo + 2 * MB, :]
-            nx = wx[lo + MB:lo + 2 * MB, :]
-            ncols = [jnp.broadcast_to(na[:, lo + j:lo + j + 1], (MB, NB)) for j in range(MB)]
+        if k + AHEAD < groups:
+            window.append(rows_of(k + AHEAD))
+        a, x = window.pop(0)
+        columns = lambda z: [jnp.broadcast_to(z[:, lo + j:lo + j + 1], (MB, NB)) for j in range(MB)]
+        cols = columns(a)
+        others = [[na, nx, columns(na)] for na, nx in window]
         inv_d = jnp.zeros((MB, NB), jnp.float32)
         piv = jnp.zeros((MB, NB), jnp.float32)
         for j in range(MB):
@@ -54,22 +58,23 @@
             recip = 1.0 / pivot
             mult = jnp.where(sub > j, cols[j] * recip, 0.0)
             ra, rx = row_of(a, j), row_of(x, j)
-            if after:
-                nmult = ncols[j] * recip
-                na = na - nmult * ra
-                nx = nx - nmult * rx
+            rcs = {l: row_of(cols[l], j) for l in range(j + 1, MB)}
+            for other in others:
+                nmult = other[2][j] * recip
+                other[0] = other[0] - nmult * ra
+                other[1] = other[1] - nmult * rx
+                for l in range(j + 1, MB):
+                    other[2][l] = other[2][l] - nmult * rcs[l]
             for l in range(j + 1, MB):
-                rc = row_of(cols[l], j)
-                cols[l] = cols[l] - mult * rc
-                if after:
-                    ncols[l] = ncols[l] - nmult * rc
+                cols[l] = cols[l] - mult * rcs[l]
             a = a - mult * ra
             x = x - mult * rx
             inv_d = jnp.where(sub == j, recip, inv_d)
             piv = jnp.where(sub == j, pivot, piv)
+        window = [(other[0], other[1]) for other in others]
         out[lo:lo + MB, :] = x * (1.0 / jnp.sqrt(piv))
-        if lo + 2 * MB < NB:
-            top = lo + 2 * MB
+        top = lo + (1 + AHEAD) * MB
+        if top < NB:
             right = jnp.concatenate([a * inv_d, x * inv_d], axis=1)
             lh, lm, ll = split3(a)
             rh, rm, rl = split3(right)
@@ -78,8 +83,6 @@
             prod = lax.dot_general(left_stack, right_stack, TN, preferred_element_type=jnp.float32)
             wa[top:, :] = wa[top:, :] - prod[top:, :NB]
             wx[top:, :] = wx[top:, :] - prod[top:, NB:]
-        if after:
-            a, x = na, nx
 
 
 def chol_panels(first, count, src, dst, big, wa, wx, linv, ys, arrive, leave):
@@ -109,36 +112,43 @@
         wx[...] = eye
         big[pl.ds(at, NB), pl.ds(at, NB)] = eye
         factor_block(wa, wx, linv)
-        y = jnp.dot(linv[...], big[pl.ds(at, NB), :], precision=lax.Precision.HIGHEST, preferred_element_type=jnp.float32)
+        ih, im, il = (part.astype(jnp.bfloat16) for part in split3(linv[...]))
+        rh, rm, rl = (part.astype(jnp.bfloat16) for part in split3(big[pl.ds(at, NB), :]))
+        mul = lambda u, v: jnp.dot(jnp.concatenate(u, axis=1), jnp.concatenate(v, axis=0), preferred_element_type=jnp.float32)
+        y = mul((ih, im), (rh, rm)) + (mul((im, ih), (rh, rm)) + mul((il, ih), (rh, rl)))
         big[pl.ds(at, NB), :] = y
         store(p).start()
         high, mid, low = (part.astype(jnp.bfloat16) for part in split3(y))
         for i, part in enumerate((high, mid, low, high)):
             ys[i * NB:(i + 1) * NB, :] = part
 
-        def trail(i, c):
-            row = pl.multiple_of(i * NB, NB)
-
-            @pl.when(p == first)
-            def _():
-                load(i).wait()
-
-            big[pl.ds(row, NB), pl.ds(at, NB)] = jnp.zeros((NB, NB), jnp.float32)
-            hm = ys[0:2 * NB, pl.ds(row, NB)]
-            mh = jnp.concatenate([ys[NB:2 * NB, pl.ds(row, NB)], ys[0:NB, pl.ds(row, NB)]], axis=0)
-            lh = ys[2 * NB:4 * NB, pl.ds(row, NB)]
+        def trail(u, c):
+            row = pl.multiple_of(u * 2 * NB, 2 * NB)
+            wide = pl.ds(row, 2 * NB)
+            hm = ys[0:2 * NB, wide]
+            mh = jnp.concatenate([ys[NB:2 * NB, wide], ys[0:NB, wide]], axis=0)
+            lh = ys[2 * NB:4 * NB, wide]
             hl = jnp.concatenate([ys[0:NB, :], ys[2 * NB:3 * NB, :]], axis=0)
             dot = lambda u, v: lax.dot_general(u, v, TN, preferred_element_type=jnp.float32)
             upd = dot(hm, ys[0:2 * NB, :]) + (dot(mh, ys[0:2 * NB, :]) + dot(lh, hl))
-            big[pl.ds(row, NB), :] = big[pl.ds(row, NB), :] - upd
-
-            @pl.when(p == last)
-            def _():
-                store(i).start()
-
+            for h in range(2):
+                i = 2 * u + h
+
+                @pl.when(jnp.logical_and(i > p, p == first))
+                def _():
+                    load(i).wait()
+
+                @pl.when(i > p)
+                def _():
+                    big[block(i), pl.ds(at, NB)] = jnp.zeros((NB, NB), jnp.float32)
+                    big[block(i), :] = big[block(i), :] - upd[h * NB:(h + 1) * NB]
+
+                @pl.when(jnp.logical_and(i > p, p == last))
+                def _():
+                    store(i).start()
             return c
 
-        lax.fori_loop(p + 1, nblk, trail, 0)
+        lax.fori_loop((p + 1) // 2, nblk // 2, trail, 0)
         return carry
 
     lax.fori_loop(first, last + 1, panel_step, 0)
@@ -180,12 +190,14 @@
         fetch.start()
         hot_ref[...] = jnp.where(lax.broadcasted_iota(jnp.int32, (frames, frames), 0) == ids_ref[...], 1.0, 0.0).astype(jnp.bfloat16)
         fetch.wait()
-        got[...] = jnp.dot(tel_ref[...].reshape(rows * 16, frames), hot_ref[...], preferred_element_type=jnp.float32).reshape(rows, 16, frames)
-        lead[...] = got[:, 0, :] * keep_ref[0:1, 0:1]
+        got[...] = tel_ref[...].astype(jnp.float32)
+        both = jnp.concatenate([got[:, 0, :], got[:, 1, :]], axis=0).astype(jnp.bfloat16)
+        both = jnp.dot(both, hot_ref[...], preferred_element_type=jnp.float32)
+        lead[...] = both[:rows] * keep_ref[0:1, 0:1]
         at = pl.multiple_of(core_ref[0] * half, half)
         mine_ref[...] = lead[pl.ds(at, half), :].astype(jnp.bfloat16)
         theirs_ref[...] = lead[pl.ds(pl.multiple_of(half - at, half), half), :].astype(jnp.bfloat16)
-        second_ref[...] = (got[:, 1, :] * keep_ref[1:2, 0:1]).astype(jnp.bfloat16)
+        second_ref[...] = (both[rows:] * keep_ref[1:2, 0:1]).astype(jnp.bfloat16)
 
     whole = lambda shape: pl.BlockSpec(shape, lambda i: (0,) * len(shape))
     shapes = ((half, frames), (half, frames), (rows, frames), (frames, frames))
@@ -231,6 +243,7 @@
     half = own[0].shape[3]
     scale = 1.0 / (tm_count * frames)
     group = 2 * RING
+    extra = 16
 
     def kernel(place_ref, *refs):
         parts = (refs[:RING], refs[RING:2 * RING])
@@ -250,13 +263,13 @@
                     for i in range(RING):
                         for q in range(RING):
                             at = x_lo * (width // 2) + ((outer_me + RING - i) % RING) * outer_step + ((inner_me + RING - q) % RING) * inner_step + by * half
-                            pltpu.make_async_copy(parts[kind][i].at[q, shift_x, shift_c], left.at[slot, pl.ds(pl.multiple_of(at, half), half)], arrive.at[slot]).start()
+                            pltpu.make_async_copy(parts[kind][i].at[q, shift_x, shift_c], left.at[slot, pl.ds(pl.multiple_of(at + extra, half), half)], arrive.at[slot]).start()
 
         def out_copy(t, slot):
-            return pltpu.make_async_copy(left.at[slot, pl.ds(0, width)], cols_hbm.at[t], leave.at[slot])
+            return pltpu.make_async_copy(left.at[slot, pl.ds(extra, width)], cols_hbm.at[t], leave.at[slot])
 
         for slot in range(2):
-            left[slot, width:, :] = jnp.zeros((16, frames), jnp.bfloat16)
+            left[slot, :extra, :] = jnp.zeros((extra, frames), jnp.bfloat16)
         fetch(0, 0)
 
         def one(t, carry):
@@ -270,31 +283,34 @@
             def _():
                 fetch(t + 1, 1 - slot)
 
-            pltpu.make_async_copy(cols_hbm.at[0], left.at[slot, pl.ds(0, width)], arrive.at[slot]).wait()
-            left[slot, width:width + quarter, :] = rows_ref[t]
+            pltpu.make_async_copy(cols_hbm.at[0], left.at[slot, pl.ds(extra, width)], arrive.at[slot]).wait()
+            left[slot, :quarter, :] = rows_ref[t]
             out_copy(t, slot).start()
-            part = lax.dot_general(left[slot], left[slot, :width, :], NT, preferred_element_type=jnp.float32)
-
-            @pl.when(t == 0)
-            def _():
-                acc[...] = part
-
-            @pl.when(t > 0)
-            def _():
-                acc[...] += part
-
+            strip = width // STRIPS
+            for s in range(STRIPS):
+                top, end = (extra + s * strip if s else 0), extra + (s + 1) * strip
+                part = lax.dot_general(left[slot, top:end, :], left[slot, extra + s * strip:, :], NT, preferred_element_type=jnp.float32)
+
+                @pl.when(t == 0)
+                def _():
+                    acc[top:end, s * strip:] = part
+
+                @pl.when(t > 0)
+                def _():
+                    acc[top:end, s * strip:] += part
             return carry
 
         lax.fori_loop(0, tm_count, one, 0)
         rows = lax.broadcasted_iota(jnp.int32, (NB, width), 0)
         cols = lax.broadcasted_iota(jnp.int32, (NB, width), 1)
         for at in range(0, width, NB):
-            acc[at:at + NB, :] = acc[at:at + NB, :] * scale + jnp.where(rows + at == cols, noise_ref[...], 0.0)
-            pltpu.make_async_copy(acc.at[pl.ds(at, NB)], gram_hbm.at[pl.ds(at, NB)], gram_sem).start()
-        second = acc[width:width + quarter, :] * scale
+            cut = pl.ds(extra + at, NB)
+            acc[cut, :] = acc[cut, :] * scale + jnp.where(rows + at == cols, noise_ref[...], 0.0)
+            pltpu.make_async_copy(acc.at[cut], gram_hbm.at[pl.ds(at, NB)], gram_sem).start()
+        second = acc[:quarter, :] * scale
         for i in range(group):
             second_ref[i] = second
-        pltpu.make_async_copy(acc.at[pl.ds(0, width)], gram_hbm, gram_sem).wait()
+        pltpu.make_async_copy(acc.at[pl.ds(extra, width)], gram_hbm, gram_sem).wait()
         out_copy(tm_count - 2, 0).wait()
         out_copy(tm_count - 1, 1).wait()
 
@@ -305,7 +321,7 @@
                    jax.ShapeDtypeStruct((group, quarter, width), jnp.float32)),
         in_specs=[SCALARS] + [anywhere] * (2 * RING) + [WHOLE] * 2,
         out_specs=(HBM, HBM, WHOLE),
-        scratch_shapes=[pltpu.VMEM((2, width + 16, frames), jnp.bfloat16), pltpu.VMEM((width + 16, width), jnp.float32),
+        scratch_shapes=[pltpu.VMEM((2, width + extra, frames), jnp.bfloat16), pltpu.VMEM((width + extra, width), jnp.float32),
                         pltpu.SemaphoreType.DMA((2,)), pltpu.SemaphoreType.DMA((2,)), pltpu.SemaphoreType.DMA],
         compiler_params=params(40), name="lead_gram")(place, *own, *other, second_rows, noise)
 

time: 257 us -> 255 us (level)
  Pallas kernels: 115 us -> 110 us
    pallas_call x3, Pallas kernels: 52.8 us -> 49.1 us  [chol_step(): pl.pallas_call(kernel, out_shape=pltpu.HBM((n, n), jnp.float32), in_specs...]
  transfers between devices with their start and end apart: 21 -> 21, of which waited for: 10 -> 10; matrix products, arithmetic and copies ran while one was open for 0% -> 0% of each run, Pallas kernels for 26% -> 24%
where the time goes in v3:
time: 255 us; the launch traced here: 253 us
  Pallas kernels  110 us (43%)
  waiting for transfers between devices  101 us (40%)
  starting transfers between devices  36.8 us (14%)
  local copies, waits for them, and re-layouts  3.06 us (1%)
    ppermute x18, waiting for transfers between devices, send(): lax.ppermute(value, AXES, [(device_id(*d), device_id(*step(*d))) for d in...  95.2 us
    pallas_call x3, Pallas kernels, chol_step(): pl.pallas_call(kernel, out_shape=pltpu.HBM((n, n), jnp.float32), in_specs...  49.1 us
    pallas_call x1, Pallas kernels, finish(): pl.pallas_call(kernel, out_shape=(out, out), grid_spec=pltpu.PrefetchScal...  29 us
    ppermute x18, starting transfers between devices, send(): lax.ppermute(value, AXES, [(device_id(*d), device_id(*step(*d))) for d in...  22.7 us
    pallas_call x1, Pallas kernels, lead_gram(): pl.pallas_call(kernel, out_shape=(pltpu.HBM((tm_count, width, frames), jn...  16.7 us
    pallas_call x1, Pallas kernels, pick_all(): pl.pallas_call(kernel, out_shape=(pltpu.HBM((quarter, cycles, frames), jn...  12.6 us
    all_to_all x1, starting transfers between devices, shards(): near = lax.all_to_all(second_gram, AXES, 0, 0, axis_index_groups=CHIP_ROWS)  6.39 us
    all_to_all x1, waiting for transfers between devices, shards(): mine2 = lax.all_to_all(near, AXES, 0, 0, axis_index_groups=PLANES)  5.98 us
  transfers between devices with their start and end apart: 21, of which 10 were waited for; matrix products, arithmetic and copies ran while one was open for 0% of the time, Pallas kernels for 24%

profile of v3, /device:TPU:0, one launch (start us, length us, event | category | flops | bytes accessed | tf_op | source)
XLA Modules:
  0.0 253.0 jit_solution(1561540833077821510)
XLA Ops:
  0.7 0.8 reshape.68
  1.5 0.7 copy-done.1
  2.2 2.4 pick_first.1
  4.7 1.2 collective-permute-done
  5.9 3.2 %collective-permute-start.2 = (bf16[2,16,1024]{2,1,0:T(8,128)(2,1)S(1)}, bf16[2,16,1024]{2,1,0:T(8,128)(2,1)S(1)}, u32[]{:S(2)}, u32[]{:S(2)}) collective-permute-start(bf16[2,16,1024]{2,1,0:T(8,128)(2,1)S(1)} %get-tuple-element.73), channel_id=1, source_target_pairs={{0,64},{32,96},{4,68},{36,100},{8,72},{40,104},{12,76},{44,108},{1... | collective-permute-start | bytes 196616 | tf_op jit(solution)/shard_map/ppermute | solution.py:454
  9.7 2.6 %collective-permute-start.3 = (bf16[2,16,1024]{2,1,0:T(8,128)(2,1)S(1)}, bf16[2,16,1024]{2,1,0:T(8,128)(2,1)S(1)}, u32[]{:S(2)}, u32[]{:S(2)}) collective-permute-start(bf16[2,16,1024]{2,1,0:T(8,128)(2,1)S(1)} %get-tuple-element.73), channel_id=1, source_target_pairs={{0,80},{32,112},{4,84},{36,116},{8,88},{40,120},{12,92},{44,124},{... | collective-permute-start | bytes 196616 | tf_op jit(solution)/shard_map/ppermute | solution.py:454
  12.4 2.2 collective-permute-done.1
  14.7 3.3 %collective-permute-start.5 = (bf16[4,2,16,1024]{3,2,1,0:T(8,128)(2,1)S(1)}, bf16[4,2,16,1024]{3,2,1,0:T(8,128)(2,1)S(1)}, u32[]{:S(2)}, u32[]{:S(2)}) collective-permute-start(bf16[4,2,16,1024]{3,2,1,0:T(8,128)(2,1)S(1)} %get-tuple-element.71), channel_id=1, source_target_pairs={{0,2},{32,40},{4,6},{36,44},{8,10},{40,32},{12,14},{44,36},{1,3},{... | collective-permute-start | bytes 786440 | tf_op jit(solution)/shard_map/ppermute | solution.py:454
  18.0 0.7 collective-permute-start.4
  18.6 2.6 %collective-permute-start.6 = (bf16[4,2,16,1024]{3,2,1,0:T(8,128)(2,1)S(1)}, bf16[4,2,16,1024]{3,2,1,0:T(8,128)(2,1)S(1)}, u32[]{:S(2)}, u32[]{:S(2)}) collective-permute-start(bf16[4,2,16,1024]{3,2,1,0:T(8,128)(2,1)S(1)} %get-tuple-element.71), channel_id=1, source_target_pairs={{0,3},{32,44},{4,7},{36,32},{8,11},{40,36},{12,15},{44,40},{1,0},{... | collective-permute-start | bytes 786440 | tf_op jit(solution)/shard_map/ppermute | solution.py:454
  21.2 1.4 collective-permute-done.5
  22.6 2.9 %collective-permute-done.4 = bf16[4,2,16,1024]{3,2,1,0:T(8,128)(2,1)S(1)} collective-permute-done((bf16[4,2,16,1024]{3,2,1,0:T(8,128)(2,1)S(1)}, bf16[4,2,16,1024]{3,2,1,0:T(8,128)(2,1)S(1)}, u32[]{:S(2)}, u32[]{:S(2)}) %collective-permute-start.4) | collective-permute-done | bytes 262176 | tf_op jit(solution)/shard_map/ppermute | solution.py:454
  25.9 4.1 %collective-permute-start.9 = (bf16[4,4,2,16,1024]{4,3,2,1,0:T(8,128)(2,1)S(1)}, bf16[4,4,2,16,1024]{4,3,2,1,0:T(8,128)(2,1)}, u32[]{:S(2)}, u32[]{:S(2)}) collective-permute-start(bf16[4,4,2,16,1024]{4,3,2,1,0:T(8,128)(2,1)S(1)} %pad_maximum_fusion.refs_0_), channel_id=1, source_target_pairs={{0,12},{32,35},{4,0},{36,39},{8,4},{40,43},{12,8},{44,47},{1,13},{... | collective-permute-start | bytes 3145736 | tf_op jit(solution)/shard_map/ppermute | solution.py:454
  30.1 1.3 collective-permute-start.7
  31.4 22.2 %collective-permute-done.9.refs_3_ = bf16[4,4,2,16,1024]{4,3,2,1,0:T(8,128)(2,1)} collective-permute-done((bf16[4,4,2,16,1024]{4,3,2,1,0:T(8,128)(2,1)S(1)}, bf16[4,4,2,16,1024]{4,3,2,1,0:T(8,128)(2,1)}, u32[]{:S(2)}, u32[]{:S(2)}) %collective-permute-start.9) | collective-permute-done | bytes 1048608 | tf_op jit(solution)/shard_map/ppermute | solution.py:454
  54.1 3.3 %collective-permute-done.7.refs_1_ = bf16[4,4,2,16,1024]{4,3,2,1,0:T(8,128)(2,1)} collective-permute-done((bf16[4,4,2,16,1024]{4,3,2,1,0:T(8,128)(2,1)S(1)}, bf16[4,4,2,16,1024]{4,3,2,1,0:T(8,128)(2,1)}, u32[]{:S(2)}, u32[]{:S(2)}) %collective-permute-start.7) | collective-permute-done | bytes 1048608 | tf_op jit(solution)/shard_map/ppermute | solution.py:454
  57.4 3.3 %all-to-all-start = ((bf16[4,8,1024]{2,1,0:T(8,128)(2,1)}), bf16[4,8,1024]{2,1,0:T(8,128)(2,1)S(1)}, u32[]{:S(2)}, u32[]{:S(2)}) async-start(bf16[4,8,1024]{2,1,0:T(8,128)(2,1)} %bitcast.17), calls=%async_computation | async-start | bytes 131072 | tf_op jit(solution)/shard_map/all_to_all | solution.py:503
  60.8 12.6 %pick_all.1 = (bf16[8,96,1024]{2,1,0:T(8,128)(2,1)}, bf16[8,96,1024]{2,1,0:T(8,128)(2,1)}, bf16[8,96,1024]{2,1,0:T(8,128)(2,1)}, bf16[8,96,1024]{2,1,0:T(8,128)(2,1)}) custom-call(s32[1]{0:T(128)} %bitcast.tm_ref, bf16[32,96,1024]{2,1,0:T(8,128)(2,1)} %bitcast.28, bf16[1024,1024]{1,0:T(8,128)(2,1)S(1)} %get-tuple-element.40.hot_ref, ...), custom_call_target="tpu_custom_call" | custom-call | tf_op jit(solution)/shard_map/pick_all/pallas_call | solution.py:230
  73.4 16.7 %lead_gram.1 = (bf16[4,1024,1024]{2,1,0:T(8,128)(2,1)}, f32[1024,1024]{1,0:T(8,128)}, f32[8,8,1024]{2,1,0:T(8,128)}) custom-call(s32[4]{0:T(128)S(1)} %pad_add_fusion.place_ref, bf16[4,4,2,16,1024]{4,3,2,1,0:T(8,128)(2,1)S(1)} %pad_maximum_fusion.refs_0_, bf16[4,4,2,16,1024]{4,3,2,1,0:T(8,128)(2,1)} %collective-permute-done.7.refs_1_, ...), custom_call_target="tpu_custom_call" | custom-call | tf_op jit(solution)/shard_map/lead_gram/pallas_call | solution.py:318
  90.2 6.4 %all-to-all-start.1 = ((f32[8,8,1024]{2,1,0:T(8,128)}), f32[8,8,1024]{2,1,0:T(8,128)S(1)}, u32[]{:S(2)}, u32[]{:S(2)}) async-start(f32[8,8,1024]{2,1,0:T(8,128)} %get-tuple-element.56), calls=%async_computation.1 | async-start | bytes 524288 | tf_op jit(solution)/shard_map/all_to_all | solution.py:509
  96.6 15.1 %chol_panels.3.src_ref = f32[1024,1024]{1,0:T(8,128)} custom-call(f32[1024,1024]{1,0:T(8,128)} %get-tuple-element.57.src_ref), custom_call_target="tpu_custom_call", output_to_operand_aliasing={{}: (0, {})} | custom-call | tf_op jit(solution)/shard_map/chol_panels/pallas_call | solution.py:170
  111.7 1.6 broadcast_in_dim.35
  113.3 4.4 %all-to-all-start.2 = ((f32[16,8,8,512]{3,2,1,0:T(8,128)}), f32[16,8,8,512]{3,2,1,0:T(8,128)S(1)}, u32[]{:S(2)}, u32[]{:S(2)}) async-start(f32[16,8,8,512]{3,2,1,0:T(8,128)} %broadcast_in_dim.35), calls=%async_computation.2 | async-start | bytes 4194304 | tf_op jit(solution)/shard_map/all_to_all | solution.py:516
  117.7 28.1 %chol_panels.4.src_ref = f32[1024,1024]{1,0:T(8,128)} custom-call(f32[1024,1024]{1,0:T(8,128)} %chol_panels.3.src_ref), custom_call_target="tpu_custom_call", output_to_operand_aliasing={{}: (0, {})} | custom-call | tf_op jit(solution)/shard_map/chol_panels/pallas_call | solution.py:170
  145.9 6.0 %all-to-all-done.2.mine_hbm = f32[16,8,8,512]{3,2,1,0:T(8,128)S(1)} async-done(((f32[16,8,8,512]{3,2,1,0:T(8,128)}), f32[16,8,8,512]{3,2,1,0:T(8,128)S(1)}, u32[]{:S(2)}, u32[]{:S(2)}) %all-to-all-start.2) | async-done | bytes 2097184 | tf_op jit(solution)/shard_map/all_to_all | solution.py:516
  151.9 2.2 collective-permute-start.15
  154.3 1.2 collective-permute-start.16
  155.5 0.7 compare_select_fusion.diag_ref
  156.2 5.9 %chol_panels.5.inv_hbm = f32[1024,1024]{1,0:T(8,128)} custom-call(f32[1024,1024]{1,0:T(8,128)} %chol_panels.4.src_ref), custom_call_target="tpu_custom_call", output_to_operand_aliasing={{}: (0, {})} | custom-call | tf_op jit(solution)/shard_map/chol_panels/pallas_call | solution.py:170
  162.1 28.9 %collective-permute-done.15.r2 = bf16[8,96,1024]{2,1,0:T(8,128)(2,1)} collective-permute-done((bf16[8,96,1024]{2,1,0:T(8,128)(2,1)}, bf16[8,96,1024]{2,1,0:T(8,128)(2,1)}, u32[]{:S(2)}, u32[]{:S(2)}) %collective-permute-start.15) | collective-permute-done | bytes 1572896 | tf_op jit(solution)/shard_map/ppermute | solution.py:454
  191.0 32.8 %collective-permute-done.16.r3 = bf16[8,96,1024]{2,1,0:T(8,128)(2,1)} collective-permute-done((bf16[8,96,1024]{2,1,0:T(8,128)(2,1)}, bf16[8,96,1024]{2,1,0:T(8,128)(2,1)}, u32[]{:S(2)}, u32[]{:S(2)}) %collective-permute-start.16) | collective-permute-done | bytes 1572896 | tf_op jit(solution)/shard_map/ppermute | solution.py:454
  223.7 29.0 %finish.1 = (f32[8,96,1024]{2,1,0:T(8,128)}, f32[8,96,1024]{2,1,0:T(8,128)}) custom-call(s32[1]{0:T(128)} %bitcast.tm_ref, bf16[8,96,1024]{2,1,0:T(8,128)(2,1)} %get-tuple-element.46.r0, bf16[8,96,1024]{2,1,0:T(8,128)(2,1)} %collective-permute-done.14.r1, bf16[8,96,1024]{2,1,0:T(8,128)(2,1)} %collective-permute-done.15.r2, ...), custom_call_target="tpu_custom_call" | custom-call | tf_op jit(solution)/shard_map/finish/pallas_call | solution.py:430
  (33 shorter events, 2.1 us)
Async XLA Ops:
  1.5 0.7 copy-start.1
  4.6 1.3 collective-permute-start
  5.9 6.5 %collective-permute-start.2 = (bf16[2,16,1024]{2,1,0:T(8,128)(2,1)S(1)}, bf16[2,16,1024]{2,1,0:T(8,128)(2,1)S(1)}, u32[]{:S(2)}, u32[]{:S(2)}) collective-permute-start(bf16[2,16,1024]{2,1,0:T(8,128)(2,1)S(1)} %get-tuple-element.73), channel_id=1, source_target_pairs={{0,64},{32,96},{4,68},{36,100},{8,72},{40,104},{12,76},{44,108},{1... | collective-permute-start | bytes 196616 | tf_op jit(solution)/shard_map/ppermute | solution.py:454
  9.2 5.5 %collective-permute-start.1 = (bf16[2,16,1024]{2,1,0:T(8,128)(2,1)S(1)}, bf16[2,16,1024]{2,1,0:T(8,128)(2,1)S(1)}, u32[]{:S(2)}, u32[]{:S(2)}) collective-permute-start(bf16[2,16,1024]{2,1,0:T(8,128)(2,1)S(1)} %get-tuple-element.73), channel_id=1, source_target_pairs={{0,16},{32,48},{4,20},{36,52},{8,24},{40,56},{12,28},{44,60},{1,17... | collective-permute-start | bytes 196616 | tf_op jit(solution)/shard_map/ppermute | solution.py:454
  9.7 4.9 %collective-permute-start.3 = (bf16[2,16,1024]{2,1,0:T(8,128)(2,1)S(1)}, bf16[2,16,1024]{2,1,0:T(8,128)(2,1)S(1)}, u32[]{:S(2)}, u32[]{:S(2)}) collective-permute-start(bf16[2,16,1024]{2,1,0:T(8,128)(2,1)S(1)} %get-tuple-element.73), channel_id=1, source_target_pairs={{0,80},{32,112},{4,84},{36,116},{8,88},{40,120},{12,92},{44,124},{... | collective-permute-start | bytes 196616 | tf_op jit(solution)/shard_map/ppermute | solution.py:454
  14.7 8.0 %collective-permute-start.5 = (bf16[4,2,16,1024]{3,2,1,0:T(8,128)(2,1)S(1)}, bf16[4,2,16,1024]{3,2,1,0:T(8,128)(2,1)S(1)}, u32[]{:S(2)}, u32[]{:S(2)}) collective-permute-start(bf16[4,2,16,1024]{3,2,1,0:T(8,128)(2,1)S(1)} %get-tuple-element.71), channel_id=1, source_target_pairs={{0,2},{32,40},{4,6},{36,44},{8,10},{40,32},{12,14},{44,36},{1,3},{... | collective-permute-start | bytes 786440 | tf_op jit(solution)/shard_map/ppermute | solution.py:454
  18.0 7.6 %collective-permute-start.4 = (bf16[4,2,16,1024]{3,2,1,0:T(8,128)(2,1)S(1)}, bf16[4,2,16,1024]{3,2,1,0:T(8,128)(2,1)S(1)}, u32[]{:S(2)}, u32[]{:S(2)}) collective-permute-start(bf16[4,2,16,1024]{3,2,1,0:T(8,128)(2,1)S(1)} %get-tuple-element.71), channel_id=1, source_target_pairs={{0,1},{32,36},{4,5},{36,40},{8,9},{40,44},{12,13},{44,32},{1,2},{3... | collective-permute-start | bytes 786440 | tf_op jit(solution)/shard_map/ppermute | solution.py:454
  18.6 7.2 %collective-permute-start.6 = (bf16[4,2,16,1024]{3,2,1,0:T(8,128)(2,1)S(1)}, bf16[4,2,16,1024]{3,2,1,0:T(8,128)(2,1)S(1)}, u32[]{:S(2)}, u32[]{:S(2)}) collective-permute-start(bf16[4,2,16,1024]{3,2,1,0:T(8,128)(2,1)S(1)} %get-tuple-element.71), channel_id=1, source_target_pairs={{0,3},{32,44},{4,7},{36,32},{8,11},{40,36},{12,15},{44,40},{1,0},{... | collective-permute-start | bytes 786440 | tf_op jit(solution)/shard_map/ppermute | solution.py:454
  25.9 27.7 %collective-permute-start.9 = (bf16[4,4,2,16,1024]{4,3,2,1,0:T(8,128)(2,1)S(1)}, bf16[4,4,2,16,1024]{4,3,2,1,0:T(8,128)(2,1)}, u32[]{:S(2)}, u32[]{:S(2)}) collective-permute-start(bf16[4,4,2,16,1024]{4,3,2,1,0:T(8,128)(2,1)S(1)} %pad_maximum_fusion.refs_0_), channel_id=1, source_target_pairs={{0,12},{32,35},{4,0},{36,39},{8,4},{40,43},{12,8},{44,47},{1,13},{... | collective-permute-start | bytes 3145736 | tf_op jit(solution)/shard_map/ppermute | solution.py:454
  30.0 23.6 %collective-permute-start.8 = (bf16[4,4,2,16,1024]{4,3,2,1,0:T(8,128)(2,1)S(1)}, bf16[4,4,2,16,1024]{4,3,2,1,0:T(8,128)(2,1)}, u32[]{:S(2)}, u32[]{:S(2)}) collective-permute-start(bf16[4,4,2,16,1024]{4,3,2,1,0:T(8,128)(2,1)S(1)} %pad_maximum_fusion.refs_0_), channel_id=1, source_target_pairs={{0,8},{32,34},{4,12},{36,38},{8,0},{40,42},{12,4},{44,46},{1,9},{3... | collective-permute-start | bytes 3145736 | tf_op jit(solution)/shard_map/ppermute | solution.py:454
  30.1 27.4 %collective-permute-start.7 = (bf16[4,4,2,16,1024]{4,3,2,1,0:T(8,128)(2,1)S(1)}, bf16[4,4,2,16,1024]{4,3,2,1,0:T(8,128)(2,1)}, u32[]{:S(2)}, u32[]{:S(2)}) collective-permute-start(bf16[4,4,2,16,1024]{4,3,2,1,0:T(8,128)(2,1)S(1)} %pad_maximum_fusion.refs_0_), channel_id=1, source_target_pairs={{0,4},{32,33},{4,8},{36,37},{8,12},{40,41},{12,0},{44,45},{1,5},{3... | collective-permute-start | bytes 3145736 | tf_op jit(solution)/shard_map/ppermute | solution.py:454
  31.4 42.0 %collective-permute-start.10 = (bf16[4,4,2,16,1024]{4,3,2,1,0:T(8,128)(2,1)S(1)}, bf16[4,4,2,16,1024]{4,3,2,1,0:T(8,128)(2,1)}, u32[]{:S(2)}, u32[]{:S(2)}) collective-permute-start(bf16[4,4,2,16,1024]{4,3,2,1,0:T(8,128)(2,1)S(1)} %pad_maximum_fusion.refs_0_), channel_id=1, source_target_pairs={{0,32},{32,0},{4,36},{36,4},{8,40},{40,8},{12,44},{44,12},{1,33},{... | collective-permute-start | bytes 3145736 | tf_op jit(solution)/shard_map/ppermute | solution.py:454
  53.6 19.8 %collective-permute-start.13 = (bf16[4,4,2,16,1024]{4,3,2,1,0:T(8,128)(2,1)}, bf16[4,4,2,16,1024]{4,3,2,1,0:T(8,128)(2,1)}, u32[]{:S(2)}, u32[]{:S(2)}) collective-permute-start(bf16[4,4,2,16,1024]{4,3,2,1,0:T(8,128)(2,1)} %collective-permute-done.9.refs_3_), channel_id=1, source_target_pairs={{0,32},{32,0},{4,36},{36,4},{8,40},{40,8},{12,44},{44,12},{1,33},{... | collective-permute-start | bytes 3145736 | tf_op jit(solution)/shard_map/ppermute | solution.py:454
  53.6 19.8 %collective-permute-start.12 = (bf16[4,4,2,16,1024]{4,3,2,1,0:T(8,128)(2,1)}, bf16[4,4,2,16,1024]{4,3,2,1,0:T(8,128)(2,1)}, u32[]{:S(2)}, u32[]{:S(2)}) collective-permute-start(bf16[4,4,2,16,1024]{4,3,2,1,0:T(8,128)(2,1)} %collective-permute-done.8.refs_2_), channel_id=1, source_target_pairs={{0,32},{32,0},{4,36},{36,4},{8,40},{40,8},{12,44},{44,12},{1,33},{... | collective-permute-start | bytes 3145736 | tf_op jit(solution)/shard_map/ppermute | solution.py:454
  57.4 16.0 %collective-permute-start.11 = (bf16[4,4,2,16,1024]{4,3,2,1,0:T(8,128)(2,1)}, bf16[4,4,2,16,1024]{4,3,2,1,0:T(8,128)(2,1)}, u32[]{:S(2)}, u32[]{:S(2)}) collective-permute-start(bf16[4,4,2,16,1024]{4,3,2,1,0:T(8,128)(2,1)} %collective-permute-done.7.refs_1_), channel_id=1, source_target_pairs={{0,32},{32,0},{4,36},{36,4},{8,40},{40,8},{12,44},{44,12},{1,33},{... | collective-permute-start | bytes 3145736 | tf_op jit(solution)/shard_map/ppermute | solution.py:454
  57.4 16.0 %all-to-all-start = ((bf16[4,8,1024]{2,1,0:T(8,128)(2,1)}), bf16[4,8,1024]{2,1,0:T(8,128)(2,1)S(1)}, u32[]{:S(2)}, u32[]{:S(2)}) async-start(bf16[4,8,1024]{2,1,0:T(8,128)(2,1)} %bitcast.17), calls=%async_computation | async-start | bytes 131072 | tf_op jit(solution)/shard_map/all_to_all | solution.py:503
  60.8 12.6 %copy-start = (f32[1024]{0:T(1024)S(1)}, f32[1024]{0:T(1024)}, u32[]{:S(2)}) copy-start(f32[1024]{0:T(1024)} %param.8) | copy-start | bytes 12292
  90.2 21.5 %all-to-all-start.1 = ((f32[8,8,1024]{2,1,0:T(8,128)}), f32[8,8,1024]{2,1,0:T(8,128)S(1)}, u32[]{:S(2)}, u32[]{:S(2)}) async-start(f32[8,8,1024]{2,1,0:T(8,128)} %get-tuple-element.56), calls=%async_computation.1 | async-start | bytes 524288 | tf_op jit(solution)/shard_map/all_to_all | solution.py:509
  113.3 38.5 %all-to-all-start.2 = ((f32[16,8,8,512]{3,2,1,0:T(8,128)}), f32[16,8,8,512]{3,2,1,0:T(8,128)S(1)}, u32[]{:S(2)}, u32[]{:S(2)}) async-start(f32[16,8,8,512]{3,2,1,0:T(8,128)} %broadcast_in_dim.35), calls=%async_computation.2 | async-start | bytes 4194304 | tf_op jit(solution)/shard_map/all_to_all | solution.py:516
  151.9 10.2 %copy-start.2 = (f32[16,8,8,512]{3,2,1,0:T(8,128)}, f32[16,8,8,512]{3,2,1,0:T(8,128)S(1)}, u32[]{:S(2)}) copy-start(f32[16,8,8,512]{3,2,1,0:T(8,128)S(1)} %all-to-all-done.2.mine_hbm) | copy-start | bytes 6291460
  151.9 71.9 %collective-permute-start.17 = (f32[16,8,8,512]{3,2,1,0:T(8,128)S(1)}, f32[16,8,8,512]{3,2,1,0:T(8,128)}, u32[]{:S(2)}, u32[]{:S(2)}) collective-permute-start(f32[16,8,8,512]{3,2,1,0:T(8,128)S(1)} %all-to-all-done.2.mine_hbm), channel_id=1, source_target_pairs={{0,32},{32,0},{4,36},{36,4},{8,40},{40,8},{12,44},{44,12},{1,33},{... | collective-permute-start | bytes 6291464 | tf_op jit(solution)/shard_map/ppermute | solution.py:454
  151.9 39.1 %collective-permute-start.15 = (bf16[8,96,1024]{2,1,0:T(8,128)(2,1)}, bf16[8,96,1024]{2,1,0:T(8,128)(2,1)}, u32[]{:S(2)}, u32[]{:S(2)}) collective-permute-start(bf16[8,96,1024]{2,1,0:T(8,128)(2,1)} %get-tuple-element.59), channel_id=1, source_target_pairs={{0,64},{32,96},{4,68},{36,100},{8,72},{40,104},{12,76},{44,108},{1... | collective-permute-start | bytes 4718600 | tf_op jit(solution)/shard_map/ppermute | solution.py:454
  154.1 36.9 %collective-permute-start.14 = (bf16[8,96,1024]{2,1,0:T(8,128)(2,1)}, bf16[8,96,1024]{2,1,0:T(8,128)(2,1)}, u32[]{:S(2)}, u32[]{:S(2)}) collective-permute-start(bf16[8,96,1024]{2,1,0:T(8,128)(2,1)} %get-tuple-element.61), channel_id=1, source_target_pairs={{0,32},{32,0},{4,36},{36,4},{8,40},{40,8},{12,44},{44,12},{1,33},{... | collective-permute-start | bytes 4718600 | tf_op jit(solution)/shard_map/ppermute | solution.py:454
  154.3 69.4 %collective-permute-start.16 = (bf16[8,96,1024]{2,1,0:T(8,128)(2,1)}, bf16[8,96,1024]{2,1,0:T(8,128)(2,1)}, u32[]{:S(2)}, u32[]{:S(2)}) collective-permute-start(bf16[8,96,1024]{2,1,0:T(8,128)(2,1)} %get-tuple-element.62), channel_id=1, source_target_pairs={{0,96},{32,64},{4,100},{36,68},{8,104},{40,72},{12,108},{44,76},{1... | collective-permute-start | bytes 4718600 | tf_op jit(solution)/shard_map/ppermute | solution.py:454
